TPU v7x, 1024 devices: a whole 4x4x32 slice. The times are simulated.
1024 devices in a mesh: gx: 32 (over z_hi, y, core), gy: 4 (over x), gz: 8 (over z_lo).
Axes of the slice: x: 4, y: 4, z: 32 (z_hi: 4, z_lo: 8; z = z_hi * 8 + z_lo), core: 2. Of those that a mesh axis runs over, the one named last changes fastest.
Arguments:
- displacement: float32 [3, 64, 32, 1024], P(None, 'gx', 'gy', 'gz'), may hold values from -6 to 6
- displacement_old: float32 [3, 64, 32, 1024], P(None, 'gx', 'gy', 'gz'), may hold values from -6 to 6
- visco_state: float32 [6, 6, 64, 32, 1024], P(None, None, 'gx', 'gy', 'gz'), may hold values from -3 to 3
- energy_max: float32 [64, 32, 1024], P('gx', 'gy', 'gz'), may hold values from 0.1 to 4
- region: int32 [64, 32, 1024], P('gx', 'gy', 'gz'), may hold values from 0 to 3
- dirichlet: int32 [64, 32, 1024], P('gx', 'gy', 'gz'), may hold values 0 or 1
- prony_moduli: float32 [4, 6], replicated, may hold values from 0.02 to 0.12
- prony_times: float32 [4, 6], replicated, may hold values from 0.05 to 50
- shear_modulus: float32 [4], replicated, may hold values from 0.5 to 2
- mullins_ratio: float32 [4], replicated, may hold values from 1.5 to 4
- mullins_scale: float32 [4], replicated, may hold values from 0.3 to 3
Outputs:
- stress: float32 [6, 64, 32, 1024], P(None, 'gx', 'gy', 'gz')
- visco_next: float32 [6, 6, 64, 32, 1024], P(None, None, 'gx', 'gy', 'gz')
- energy_next: float32 [64, 32, 1024], P('gx', 'gy', 'gz')
- damage_field: float32 [64, 32, 1024], P('gx', 'gy', 'gz')
- residual: float32 [64, 32, 1024], P('gx', 'gy', 'gz')
All inputs are finite; a program needn't handle non-finite values. No bound on the sum of `dirichlet` on one device may be relied on, other than what follows from the above.
Results may differ from a plain program's by a relative error of at most 0.0003.
Values sent between devices are 32-bit elements; how exact they have to be, the bound alone decides.
A program may use at most 32 MiB of HBM per device.

v0:
```python
import functools

import jax
import jax.numpy as jnp
from jax import lax
from jax.sharding import Mesh
from jax.sharding import PartitionSpec as P

ITERS = 4
GX = ("gx_0", "gx_1", "gx_2")
GX_GY_GZ = ("gx_0", "gx_1", "gx_2", "gy", "gz")


LENGTH_SQUARED = 4.0


def extended(shard, sides, width):
    for axis, dim in sides:
        count, length = (lax.axis_size(axis), shard.shape[dim])
        up = [(i, (i + 1) % count) for i in range(count)]
        down = [(j, i) for i, j in up]
        last = lax.slice_in_dim(shard, length - width, length, axis=dim)
        leading = lax.slice_in_dim(shard, 0, width, axis=dim)
        before = lax.ppermute(last, axis, up)
        after = lax.ppermute(leading, axis, down)
        shard = jnp.concatenate([before, shard, after], axis=dim)
    return shard


def padded(shard, sides, width):
    edges = {}
    for axis, dim in sides:
        count, length = (lax.axis_size(axis), shard.shape[dim])
        up = [(i, (i + 1) % count) for i in range(count - 1)]
        last = lax.slice_in_dim(shard, length - width, length, axis=dim)
        leading = lax.slice_in_dim(shard, 0, width, axis=dim)
        edges[dim] = (
            lax.ppermute(last, axis, up),
            lax.ppermute(leading, axis, [(b, a) for a, b in up]),
        )
    done = []
    for _, dim in sides:
        low, high = edges[dim]
        around = [(width, width) if d in done else (0, 0) for d in range(shard.ndim)]
        shard = jnp.concatenate([jnp.pad(low, around), shard, jnp.pad(high, around)], axis=dim)
        done.append(dim)
    return shard


def by_axis(shard, axes):
    return functools.reduce(lax.psum, axes, shard)


def neighbours(field):
    cycle_ext = extended(field, ((GX, 1),), 1)
    slab_ext = padded(field, (("gy", 2), ("gz", 3)), 1)
    next_x = cycle_ext[:, 2:]
    prev_x = cycle_ext[:, :-2]
    next_y = slab_ext[:, :, 2:, 1:-1]
    prev_y = slab_ext[:, :, :-2, 1:-1]
    next_z = slab_ext[:, :, 1:-1, 2:]
    prev_z = slab_ext[:, :, 1:-1, :-2]
    return (next_x, prev_x, next_y, prev_y, next_z, prev_z)


def deviator(grad_x, grad_y, grad_z):
    strain_xx = grad_x[0]
    strain_yy = grad_y[1]
    strain_zz = grad_z[2]
    strain_yz = 0.5 * (grad_z[1] + grad_y[2])
    strain_xz = 0.5 * (grad_z[0] + grad_x[2])
    strain_xy = 0.5 * (grad_y[0] + grad_x[1])
    trace_third = (strain_xx + strain_yy + strain_zz) / 3.0
    return jnp.stack(
        [
            strain_xx - trace_third,
            strain_yy - trace_third,
            strain_zz - trace_third,
            strain_yz,
            strain_xz,
            strain_xy,
        ]
    )


def contract(dev):
    return (
        dev[0] * dev[0]
        + dev[1] * dev[1]
        + dev[2] * dev[2]
        + 2.0 * (dev[3] * dev[3] + dev[4] * dev[4] + dev[5] * dev[5])
    )


def operate(field):
    next_x, prev_x, next_y, prev_y, next_z, prev_z = neighbours(field)
    beside_all = next_x + prev_x + next_y + prev_y + next_z + prev_z
    return (1.0 + 6.0 * LENGTH_SQUARED) * field - LENGTH_SQUARED * beside_all


def lookup_one(table_rows, onehot):
    return jnp.sum(table_rows[:, None, None, None] * onehot, axis=0)


def lookup_many(table_rows, onehot):
    return jnp.einsum("rk,rxyz->kxyz", table_rows, onehot, precision=lax.Precision.HIGHEST)


def on_device(
    displacement,
    displacement_old,
    visco_state,
    energy_max,
    region,
    dirichlet,
    prony_moduli,
    prony_times,
    shear_modulus,
    mullins_ratio,
    mullins_scale,
):
    free_share = (1 - dirichlet).astype(jnp.float32)
    stacked = jnp.concatenate([displacement, displacement_old], axis=0) * free_share[None]
    next_x, prev_x, next_y, prev_y, next_z, prev_z = neighbours(stacked)
    grad_x = 0.5 * (next_x - prev_x)
    grad_y = 0.5 * (next_y - prev_y)
    grad_z = 0.5 * (next_z - prev_z)
    dev_new = deviator(grad_x[0:3], grad_y[0:3], grad_z[0:3])
    dev_old = deviator(grad_x[3:6], grad_y[3:6], grad_z[3:6])
    region_count = prony_moduli.shape[0]
    labels = lax.broadcasted_iota(jnp.int32, (region_count, 1, 1, 1), 0)
    onehot = (region[None] == labels).astype(jnp.float32)
    shear_cells = lookup_one(shear_modulus, onehot)
    ratio_cells = lookup_one(mullins_ratio, onehot)
    scale_cells = lookup_one(mullins_scale, onehot)
    moduli_cells = lookup_many(prony_moduli, onehot)
    times_cells = lookup_many(prony_times, onehot)
    energy = shear_cells * contract(dev_new)
    energy_next = jnp.maximum(energy_max, energy)
    softening = 1.0 - jax.scipy.special.erf((energy_next - energy) / scale_cells) / ratio_cells
    stress_jump = 2.0 * shear_cells * (dev_new - dev_old)
    decays = jnp.exp(-1.0 / times_cells)
    weight = moduli_cells * (1.0 - decays) * times_cells
    visco_next = decays[:, None] * visco_state + weight[:, None] * stress_jump[None]
    long_term = 1.0 - lookup_one(jnp.sum(prony_moduli, axis=1), onehot)
    stress = softening * (long_term * 2.0 * shear_cells * dev_new + jnp.sum(visco_next, axis=0))
    local_drive = (softening * energy)[None]
    damage_field = jnp.zeros_like(local_drive)
    residual = local_drive
    image_res = operate(residual)
    direction = residual
    image_dir = image_res
    image_two = image_res
    gamma_old = None
    alpha_old = None
    for iteration in range(ITERS):
        gamma_now, delta_now = (
            by_axis(jnp.sum(residual * residual), GX_GY_GZ),
            by_axis(jnp.sum(image_res * residual), GX_GY_GZ),
        )
        last_turn = iteration + 1 == ITERS
        if not last_turn:
            applied = operate(image_res)
        if iteration == 0:
            alpha_now = gamma_now / delta_now
            direction = residual
            image_dir = image_res
            image_two = applied
        else:
            beta_now = gamma_now / gamma_old
            alpha_now = gamma_now / (delta_now - beta_now * gamma_now / alpha_old)
            direction = residual + beta_now * direction
            image_dir = image_res + beta_now * image_dir
            if not last_turn:
                image_two = applied + beta_now * image_two
        damage_field = damage_field + alpha_now * direction
        residual = residual - alpha_now * image_dir
        if not last_turn:
            image_res = image_res - alpha_now * image_two
        gamma_old = gamma_now
        alpha_old = alpha_now
    return (stress, visco_next, energy_next, damage_field[0], residual[0])


def solution(mesh):
    split = Mesh(
        mesh.devices.reshape(4, 4, 2, mesh.shape["gy"], mesh.shape["gz"]),
        ("gx_0", "gx_1", "gx_2", "gy", "gz"),
    )
    return jax.shard_map(
        on_device,
        mesh=split,
        in_specs=(
            P(None, GX, "gy", "gz"),
            P(None, GX, "gy", "gz"),
            P(None, None, GX, "gy", "gz"),
            P(GX, "gy", "gz"),
            P(GX, "gy", "gz"),
            P(GX, "gy", "gz"),
            P(),
            P(),
            P(),
            P(),
            P(),
        ),
        out_specs=(
            P(None, GX, "gy", "gz"),
            P(None, None, GX, "gy", "gz"),
            P(GX, "gy", "gz"),
            P(GX, "gy", "gz"),
            P(GX, "gy", "gz"),
        ),
        check_vma=False,
    )
```

profile of v0, /device:TPU:1, one launch (start us, length us, event | category | flops | bytes accessed | tf_op | source)
XLA Modules:
  0.0 466.2 jit_solution(15064274134033797973)
XLA Ops:
  2.1 3.9 collective-permute-start.3
  6.1 1.3 collective-permute-start.2
  7.4 3.5 collective-permute-start.5
  11.0 1.3 collective-permute-start.4
  12.3 4.3 collective-permute-start.1
  17.3 8.7 %collective-permute-start = (f32[6,1,8,128]{3,2,1,0:T(8,128)S(1)}, f32[6,1,8,128]{3,2,1,0:T(8,128)S(1)}, u32[]{:S(2)}, u32[]{:S(2)}) collective-permute-start(f32[6,1,8,128]{3,2,1,0:T(8,128)S(1)} %get-tuple-element.95), channel_id=1, source_target_pairs={{32,0},{64,32},{96,64},{128,96},{160,128},{192,160},{224,192},{256... | collective-permute-start | bytes 73736 | tf_op jit(solution)/shard_map/ppermute | solution.py:25
  30.3 4.9 %collective-permute-start.9 = (f32[1,2,1,128]{3,2,1,0:T(1,128)S(1)}, f32[1,2,1,128]{3,2,1,0:T(1,128)S(1)}, u32[]{:S(2)}, u32[]{:S(2)}) collective-permute-start(f32[1,2,1,128]{3,2,1,0:T(1,128)S(1)} %get-tuple-element.121), channel_id=1, source_target_pairs={{0,8},{8,16},{16,24},{1,9},{9,17},{17,25},{2,10},{10,18},{18,26},{... | collective-permute-start | bytes 3080 | tf_op jit(solution)/shard_map/ppermute | solution.py:38
  35.2 4.3 collective-permute-start.11
  39.5 1.3 collective-permute-start.10
  40.8 1.9 collective-permute-start.7
  43.6 16.1 %collective-permute-start.6 = (f32[1,1,8,128]{3,2,1,0:T(8,128)S(1)}, f32[1,1,8,128]{3,2,1,0:T(8,128)S(1)}, u32[]{:S(2)}, u32[]{:S(2)}) collective-permute-start(f32[1,1,8,128]{3,2,1,0:T(8,128)S(1)} %get-tuple-element.117), channel_id=1, source_target_pairs={{32,0},{64,32},{96,64},{128,96},{160,128},{192,160},{224,192},{256... | collective-permute-start | bytes 12296 | tf_op jit(solution)/shard_map/ppermute | solution.py:25
  61.3 1.9 collective-permute-start.13
  63.2 15.0 %collective-permute-start.12 = (f32[1,1,8,128]{3,2,1,0:T(8,128)S(1)}, f32[1,1,8,128]{3,2,1,0:T(8,128)S(1)}, u32[]{:S(2)}, u32[]{:S(2)}) collective-permute-start(f32[1,1,8,128]{3,2,1,0:T(8,128)S(1)} %get-tuple-element.111), channel_id=1, source_target_pairs={{32,0},{64,32},{96,64},{128,96},{160,128},{192,160},{224,192},{256... | collective-permute-start | bytes 12296 | tf_op jit(solution)/shard_map/ppermute | solution.py:25
  78.2 1.3 collective-permute-start.14
  79.5 4.3 collective-permute-start.15
  83.8 4.3 collective-permute-start.17
  88.0 25.7 %all-reduce.25 = (f32[]{:T(128)}, f32[]{:T(128)}) all-reduce(f32[]{:T(128)} %get-tuple-element.64, f32[]{:T(128)} %get-tuple-element.62), channel_id=1, replica_groups=mesh['gx_0'=4,'gx_1'=4,'gx_2'=2,'gy'=4,'gz'=8] {'gx_0'}, use_global_device_ids=true, to_apply=%region_7.8 | all-reduce | flops 2 | bytes 16 | tf_op jit(solution)/shard_map/psum | solution.py:51
  113.8 15.5 %all-reduce.21 = (f32[]{:T(128)}, f32[]{:T(128)}) all-reduce(f32[]{:T(128)} %get-tuple-element.45, f32[]{:T(128)} %get-tuple-element.46), channel_id=1, replica_groups=mesh['gx_0'=4,'gx_1'=4,'gx_2'=2,'gy'=4,'gz'=8] {'gx_1'}, use_global_device_ids=true, to_apply=%region_8.9 | all-reduce | flops 2 | bytes 16 | tf_op jit(solution)/shard_map/psum | solution.py:51
  129.3 10.6 %all-reduce.29 = (f32[]{:T(128)}, f32[]{:T(128)}) all-reduce(f32[]{:T(128)} %get-tuple-element.37, f32[]{:T(128)} %get-tuple-element.38), channel_id=1, replica_groups=mesh['gx_0'=4,'gx_1'=4,'gx_2'=2,'gy'=4,'gz'=8] {'gx_2'}, use_global_device_ids=true, to_apply=%region_9.10 | all-reduce | flops 2 | bytes 16 | tf_op jit(solution)/shard_map/psum | solution.py:51
  139.9 8.3 %all-reduce.17 = (f32[]{:T(128)}, f32[]{:T(128)}) all-reduce(f32[]{:T(128)} %get-tuple-element.53, f32[]{:T(128)} %get-tuple-element.54), channel_id=1, replica_groups=mesh['gx_0'=4,'gx_1'=4,'gx_2'=2,'gy'=4,'gz'=8] {'gy'}, use_global_device_ids=true, to_apply=%region_10.11 | all-reduce | flops 2 | bytes 16 | tf_op jit(solution)/shard_map/psum | solution.py:51
  148.3 24.2 %all-reduce.13 = (f32[]{:T(128)}, f32[]{:T(128)}) all-reduce(f32[]{:T(128)} %get-tuple-element.29, f32[]{:T(128)} %get-tuple-element.30), channel_id=1, replica_groups=mesh['gx_0'=4,'gx_1'=4,'gx_2'=2,'gy'=4,'gz'=8] {'gz'}, use_global_device_ids=true, to_apply=%region_11.12 | all-reduce | flops 2 | bytes 16 | tf_op jit(solution)/shard_map/psum | solution.py:51
  175.1 2.1 collective-permute-done.16
  178.1 10.5 %collective-permute-start.19 = (f32[1,1,8,128]{3,2,1,0:T(8,128)S(1)}, f32[1,1,8,128]{3,2,1,0:T(8,128)S(1)}, u32[]{:S(2)}, u32[]{:S(2)}) collective-permute-start(f32[1,1,8,128]{3,2,1,0:T(8,128)S(1)} %get-tuple-element.106), channel_id=1, source_target_pairs={{0,32},{32,64},{64,96},{96,128},{128,160},{160,192},{192,224},{224... | collective-permute-start | bytes 12296 | tf_op jit(solution)/shard_map/ppermute | solution.py:24
  188.5 1.9 collective-permute-start.18
  190.5 1.3 collective-permute-start.20
  191.8 4.0 collective-permute-start.21
  195.8 20.2 %all-reduce.24 = (f32[]{:T(128)}, f32[]{:T(128)}) all-reduce(f32[]{:T(128)} %get-tuple-element.8, f32[]{:T(128)} %get-tuple-element.7), channel_id=1, replica_groups=mesh['gx_0'=4,'gx_1'=4,'gx_2'=2,'gy'=4,'gz'=8] {'gx_0'}, use_global_device_ids=true, to_apply=%region_19.20 | all-reduce | flops 2 | bytes 16 | tf_op jit(solution)/shard_map/psum | solution.py:51
  216.0 11.7 %all-reduce.20 = (f32[]{:T(128)}, f32[]{:T(128)}) all-reduce(f32[]{:T(128)} %get-tuple-element.43, f32[]{:T(128)} %get-tuple-element.44), channel_id=1, replica_groups=mesh['gx_0'=4,'gx_1'=4,'gx_2'=2,'gy'=4,'gz'=8] {'gx_1'}, use_global_device_ids=true, to_apply=%region_20.21 | all-reduce | flops 2 | bytes 16 | tf_op jit(solution)/shard_map/psum | solution.py:51
  227.7 13.0 %all-reduce.28 = (f32[]{:T(128)}, f32[]{:T(128)}) all-reduce(f32[]{:T(128)} %get-tuple-element.35, f32[]{:T(128)} %get-tuple-element.36), channel_id=1, replica_groups=mesh['gx_0'=4,'gx_1'=4,'gx_2'=2,'gy'=4,'gz'=8] {'gx_2'}, use_global_device_ids=true, to_apply=%region_21.22 | all-reduce | flops 2 | bytes 16 | tf_op jit(solution)/shard_map/psum | solution.py:51
  240.7 7.3 %all-reduce.16 = (f32[]{:T(128)}, f32[]{:T(128)}) all-reduce(f32[]{:T(128)} %get-tuple-element.51, f32[]{:T(128)} %get-tuple-element.52), channel_id=1, replica_groups=mesh['gx_0'=4,'gx_1'=4,'gx_2'=2,'gy'=4,'gz'=8] {'gy'}, use_global_device_ids=true, to_apply=%region_22.23 | all-reduce | flops 2 | bytes 16 | tf_op jit(solution)/shard_map/psum | solution.py:51
  247.9 22.3 %all-reduce.12 = (f32[]{:T(128)}, f32[]{:T(128)}) all-reduce(f32[]{:T(128)} %get-tuple-element.27, f32[]{:T(128)} %get-tuple-element.28), channel_id=1, replica_groups=mesh['gx_0'=4,'gx_1'=4,'gx_2'=2,'gy'=4,'gz'=8] {'gz'}, use_global_device_ids=true, to_apply=%region_23.24 | all-reduce | flops 2 | bytes 16 | tf_op jit(solution)/shard_map/psum | solution.py:51
  273.6 3.3 collective-permute-start.23
  279.7 2.7 collective-permute-done.22
  283.1 11.7 %collective-permute-start.25 = (f32[1,1,8,128]{3,2,1,0:T(8,128)S(1)}, f32[1,1,8,128]{3,2,1,0:T(8,128)S(1)}, u32[]{:S(2)}, u32[]{:S(2)}) collective-permute-start(f32[1,1,8,128]{3,2,1,0:T(8,128)S(1)} %get-tuple-element.100), channel_id=1, source_target_pairs={{0,32},{32,64},{64,96},{96,128},{128,160},{160,192},{192,224},{224... | collective-permute-start | bytes 12296 | tf_op jit(solution)/shard_map/ppermute | solution.py:24
  294.8 1.9 collective-permute-start.24
  296.7 1.3 collective-permute-start.26
  298.0 4.0 collective-permute-start.27
  302.0 18.3 %all-reduce.23 = (f32[]{:T(128)}, f32[]{:T(128)}) all-reduce(f32[]{:T(128)} %get-tuple-element.10, f32[]{:T(128)} %get-tuple-element.9), channel_id=1, replica_groups=mesh['gx_0'=4,'gx_1'=4,'gx_2'=2,'gy'=4,'gz'=8] {'gx_0'}, use_global_device_ids=true, to_apply=%region_31.32 | all-reduce | flops 2 | bytes 16 | tf_op jit(solution)/shard_map/psum | solution.py:51
  320.4 13.3 %all-reduce.19 = (f32[]{:T(128)}, f32[]{:T(128)}) all-reduce(f32[]{:T(128)} %get-tuple-element.41, f32[]{:T(128)} %get-tuple-element.42), channel_id=1, replica_groups=mesh['gx_0'=4,'gx_1'=4,'gx_2'=2,'gy'=4,'gz'=8] {'gx_1'}, use_global_device_ids=true, to_apply=%region_32.33 | all-reduce | flops 2 | bytes 16 | tf_op jit(solution)/shard_map/psum | solution.py:51
  333.6 11.3 %all-reduce.27 = (f32[]{:T(128)}, f32[]{:T(128)}) all-reduce(f32[]{:T(128)} %get-tuple-element.33, f32[]{:T(128)} %get-tuple-element.34), channel_id=1, replica_groups=mesh['gx_0'=4,'gx_1'=4,'gx_2'=2,'gy'=4,'gz'=8] {'gx_2'}, use_global_device_ids=true, to_apply=%region_33.34 | all-reduce | flops 2 | bytes 16 | tf_op jit(solution)/shard_map/psum | solution.py:51
  344.9 7.5 %all-reduce.15 = (f32[]{:T(128)}, f32[]{:T(128)}) all-reduce(f32[]{:T(128)} %get-tuple-element.49, f32[]{:T(128)} %get-tuple-element.50), channel_id=1, replica_groups=mesh['gx_0'=4,'gx_1'=4,'gx_2'=2,'gy'=4,'gz'=8] {'gy'}, use_global_device_ids=true, to_apply=%region_34.35 | all-reduce | flops 2 | bytes 16 | tf_op jit(solution)/shard_map/psum | solution.py:51
  352.4 24.2 %all-reduce.11 = (f32[]{:T(128)}, f32[]{:T(128)}) all-reduce(f32[]{:T(128)} %get-tuple-element.25, f32[]{:T(128)} %get-tuple-element.26), channel_id=1, replica_groups=mesh['gx_0'=4,'gx_1'=4,'gx_2'=2,'gy'=4,'gz'=8] {'gz'}, use_global_device_ids=true, to_apply=%region_35.36 | all-reduce | flops 2 | bytes 16 | tf_op jit(solution)/shard_map/psum | solution.py:51
  383.4 2.7 collective-permute-done.28
  386.8 20.2 %all-reduce.22 = (f32[]{:T(128)}, f32[]{:T(128)}) all-reduce(f32[]{:T(128)} %get-tuple-element.6, f32[]{:T(128)} %get-tuple-element.5), channel_id=1, replica_groups=mesh['gx_0'=4,'gx_1'=4,'gx_2'=2,'gy'=4,'gz'=8] {'gx_0'}, use_global_device_ids=true, to_apply=%region_43.44 | all-reduce | flops 2 | bytes 16 | tf_op jit(solution)/shard_map/psum | solution.py:51
  407.0 8.6 %all-reduce.18 = (f32[]{:T(128)}, f32[]{:T(128)}) all-reduce(f32[]{:T(128)} %get-tuple-element.39, f32[]{:T(128)} %get-tuple-element.40), channel_id=1, replica_groups=mesh['gx_0'=4,'gx_1'=4,'gx_2'=2,'gy'=4,'gz'=8] {'gx_1'}, use_global_device_ids=true, to_apply=%region_44.45 | all-reduce | flops 2 | bytes 16 | tf_op jit(solution)/shard_map/psum | solution.py:51
  415.6 14.7 %all-reduce.26 = (f32[]{:T(128)}, f32[]{:T(128)}) all-reduce(f32[]{:T(128)} %get-tuple-element.31, f32[]{:T(128)} %get-tuple-element.32), channel_id=1, replica_groups=mesh['gx_0'=4,'gx_1'=4,'gx_2'=2,'gy'=4,'gz'=8] {'gx_2'}, use_global_device_ids=true, to_apply=%region_45.46 | all-reduce | flops 2 | bytes 16 | tf_op jit(solution)/shard_map/psum | solution.py:51
  430.4 7.2 %all-reduce.14 = (f32[]{:T(128)}, f32[]{:T(128)}) all-reduce(f32[]{:T(128)} %get-tuple-element.47, f32[]{:T(128)} %get-tuple-element.48), channel_id=1, replica_groups=mesh['gx_0'=4,'gx_1'=4,'gx_2'=2,'gy'=4,'gz'=8] {'gy'}, use_global_device_ids=true, to_apply=%region_46.47 | all-reduce | flops 2 | bytes 16 | tf_op jit(solution)/shard_map/psum | solution.py:51
  437.6 24.0 %all-reduce.10 = (f32[]{:T(128)}, f32[]{:T(128)}) all-reduce(f32[]{:T(128)} %get-tuple-element.23, f32[]{:T(128)} %get-tuple-element.24), channel_id=1, replica_groups=mesh['gx_0'=4,'gx_1'=4,'gx_2'=2,'gy'=4,'gz'=8] {'gz'}, use_global_device_ids=true, to_apply=%region_47.48 | all-reduce | flops 2 | bytes 16 | tf_op jit(solution)/shard_map/psum | solution.py:51
  (87 shorter events, 17.1 us)
Async XLA Ops:
  0.6 16.0 %copy-start = (f32[4,6]{1,0:T(4,128)S(1)}, f32[4,6]{1,0:T(4,128)}, u32[]{:S(2)}) copy-start(f32[4,6]{1,0:T(4,128)} %param.18) | copy-start | bytes 292
  2.1 24.1 %collective-permute-start.3 = (f32[6,2,1,128]{3,2,1,0:T(1,128)S(1)}, f32[6,2,1,128]{3,2,1,0:T(1,128)S(1)}, u32[]{:S(2)}, u32[]{:S(2)}) collective-permute-start(f32[6,2,1,128]{3,2,1,0:T(1,128)S(1)} %get-tuple-element.93), channel_id=1, source_target_pairs={{0,8},{8,16},{16,24},{1,9},{9,17},{17,25},{2,10},{10,18},{18,26},{... | collective-permute-start | bytes 18440 | tf_op jit(solution)/shard_map/ppermute | solution.py:38
  6.1 20.2 %collective-permute-start.2 = (f32[6,2,1,128]{3,2,1,0:T(1,128)S(1)}, f32[6,2,1,128]{3,2,1,0:T(1,128)S(1)}, u32[]{:S(2)}, u32[]{:S(2)}) collective-permute-start(f32[6,2,1,128]{3,2,1,0:T(1,128)S(1)} %get-tuple-element.94), channel_id=1, source_target_pairs={{8,0},{16,8},{24,16},{9,1},{17,9},{25,17},{10,2},{18,10},{26,18},{... | collective-permute-start | bytes 18440 | tf_op jit(solution)/shard_map/ppermute | solution.py:39
  7.4 9.9 %collective-permute-start.5 = (f32[6,2,8,1]{3,2,1,0:T(8,128)S(1)}, f32[6,2,8,1]{3,2,1,0:T(8,128)S(1)}, u32[]{:S(2)}, u32[]{:S(2)}) collective-permute-start(f32[6,2,8,1]{3,2,1,0:T(8,128)S(1)} %get-tuple-element.92), channel_id=1, source_target_pairs={{0,1},{1,2},{2,3},{3,4},{4,5},{5,6},{6,7},{8,9},{9,10},{10,11},{11... | collective-permute-start | bytes 1160 | tf_op jit(solution)/shard_map/ppermute | solution.py:38
  11.0 5.7 %copy-start.2 = (s32[2,8,128]{2,1,0:T(8,128)S(1)}, s32[2,8,128]{2,1,0:T(8,128)}, u32[]{:S(2)}) copy-start(s32[2,8,128]{2,1,0:T(8,128)} %param.15) | copy-start | bytes 24580
  11.0 15.3 %collective-permute-start.4 = (f32[6,2,8,1]{3,2,1,0:T(8,128)S(1)}, f32[6,2,8,1]{3,2,1,0:T(8,128)S(1)}, u32[]{:S(2)}, u32[]{:S(2)}) collective-permute-start(f32[6,2,8,1]{3,2,1,0:T(8,128)S(1)} %get-tuple-element.91), channel_id=1, source_target_pairs={{1,0},{2,1},{3,2},{4,3},{5,4},{6,5},{7,6},{9,8},{10,9},{11,10},{12... | collective-permute-start | bytes 1160 | tf_op jit(solution)/shard_map/ppermute | solution.py:39
  12.3 4.6 copy-start.4
  12.3 14.0 %collective-permute-start.1 = (f32[6,1,8,128]{3,2,1,0:T(8,128)S(1)}, f32[6,1,8,128]{3,2,1,0:T(8,128)S(1)}, u32[]{:S(2)}, u32[]{:S(2)}) collective-permute-start(f32[6,1,8,128]{3,2,1,0:T(8,128)S(1)} %get-tuple-element.96), channel_id=1, source_target_pairs={{0,32},{32,64},{64,96},{96,128},{128,160},{160,192},{192,224},{224... | collective-permute-start | bytes 73736 | tf_op jit(solution)/shard_map/ppermute | solution.py:24
  17.3 8.8 %copy-start.5 = (f32[4]{0:T(128)S(1)}, f32[4]{0:T(128)}, u32[]{:S(2)}) copy-start(f32[4]{0:T(128)} %param.21) | copy-start | bytes 52
  17.3 8.8 %copy-start.6 = (f32[4]{0:T(128)S(1)}, f32[4]{0:T(128)}, u32[]{:S(2)}) copy-start(f32[4]{0:T(128)} %param.20) | copy-start | bytes 52
  17.3 8.8 %copy-start.7 = (f32[4]{0:T(128)S(1)}, f32[4]{0:T(128)}, u32[]{:S(2)}) copy-start(f32[4]{0:T(128)} %param.19) | copy-start | bytes 52
  17.3 9.6 %collective-permute-start = (f32[6,1,8,128]{3,2,1,0:T(8,128)S(1)}, f32[6,1,8,128]{3,2,1,0:T(8,128)S(1)}, u32[]{:S(2)}, u32[]{:S(2)}) collective-permute-start(f32[6,1,8,128]{3,2,1,0:T(8,128)S(1)} %get-tuple-element.95), channel_id=1, source_target_pairs={{32,0},{64,32},{96,64},{128,96},{160,128},{192,160},{224,192},{256... | collective-permute-start | bytes 73736 | tf_op jit(solution)/shard_map/ppermute | solution.py:25
  27.1 0.7 copy-start.3
  27.1 15.7 %copy-start.1 = (f32[6,6,2,8,128]{4,3,2,1,0:T(8,128)S(1)}, f32[6,6,2,8,128]{4,3,2,1,0:T(8,128)}, u32[]{:S(2)}) copy-start(f32[6,6,2,8,128]{4,3,2,1,0:T(8,128)} %param.13) | copy-start | bytes 884740
  29.0 31.3 %collective-permute-start.8 = (f32[1,2,1,128]{3,2,1,0:T(1,128)S(1)}, f32[1,2,1,128]{3,2,1,0:T(1,128)S(1)}, u32[]{:S(2)}, u32[]{:S(2)}) collective-permute-start(f32[1,2,1,128]{3,2,1,0:T(1,128)S(1)} %get-tuple-element.122), channel_id=1, source_target_pairs={{8,0},{16,8},{24,16},{9,1},{17,9},{25,17},{10,2},{18,10},{26,18},{... | collective-permute-start | bytes 3080 | tf_op jit(solution)/shard_map/ppermute | solution.py:39
  30.3 30.0 %collective-permute-start.9 = (f32[1,2,1,128]{3,2,1,0:T(1,128)S(1)}, f32[1,2,1,128]{3,2,1,0:T(1,128)S(1)}, u32[]{:S(2)}, u32[]{:S(2)}) collective-permute-start(f32[1,2,1,128]{3,2,1,0:T(1,128)S(1)} %get-tuple-element.121), channel_id=1, source_target_pairs={{0,8},{8,16},{16,24},{1,9},{9,17},{17,25},{2,10},{10,18},{18,26},{... | collective-permute-start | bytes 3080 | tf_op jit(solution)/shard_map/ppermute | solution.py:38
  35.2 8.4 %collective-permute-start.11 = (f32[1,2,8,1]{3,2,1,0:T(8,128)S(1)}, f32[1,2,8,1]{3,2,1,0:T(8,128)S(1)}, u32[]{:S(2)}, u32[]{:S(2)}) collective-permute-start(f32[1,2,8,1]{3,2,1,0:T(8,128)S(1)} %get-tuple-element.120), channel_id=1, source_target_pairs={{0,1},{1,2},{2,3},{3,4},{4,5},{5,6},{6,7},{8,9},{9,10},{10,11},{11... | collective-permute-start | bytes 200 | tf_op jit(solution)/shard_map/ppermute | solution.py:38
  39.5 20.8 %collective-permute-start.10 = (f32[1,2,8,1]{3,2,1,0:T(8,128)S(1)}, f32[1,2,8,1]{3,2,1,0:T(8,128)S(1)}, u32[]{:S(2)}, u32[]{:S(2)}) collective-permute-start(f32[1,2,8,1]{3,2,1,0:T(8,128)S(1)} %get-tuple-element.119), channel_id=1, source_target_pairs={{1,0},{2,1},{3,2},{4,3},{5,4},{6,5},{7,6},{9,8},{10,9},{11,10},{12... | collective-permute-start | bytes 200 | tf_op jit(solution)/shard_map/ppermute | solution.py:39
  40.8 19.6 %collective-permute-start.7 = (f32[1,1,8,128]{3,2,1,0:T(8,128)S(1)}, f32[1,1,8,128]{3,2,1,0:T(8,128)S(1)}, u32[]{:S(2)}, u32[]{:S(2)}) collective-permute-start(f32[1,1,8,128]{3,2,1,0:T(8,128)S(1)} %get-tuple-element.118), channel_id=1, source_target_pairs={{0,32},{32,64},{64,96},{96,128},{128,160},{160,192},{192,224},{224... | collective-permute-start | bytes 12296 | tf_op jit(solution)/shard_map/ppermute | solution.py:24
  43.6 16.9 %collective-permute-start.6 = (f32[1,1,8,128]{3,2,1,0:T(8,128)S(1)}, f32[1,1,8,128]{3,2,1,0:T(8,128)S(1)}, u32[]{:S(2)}, u32[]{:S(2)}) collective-permute-start(f32[1,1,8,128]{3,2,1,0:T(8,128)S(1)} %get-tuple-element.117), channel_id=1, source_target_pairs={{32,0},{64,32},{96,64},{128,96},{160,128},{192,160},{224,192},{256... | collective-permute-start | bytes 12296 | tf_op jit(solution)/shard_map/ppermute | solution.py:25
  61.3 115.9 %collective-permute-start.13 = (f32[1,1,8,128]{3,2,1,0:T(8,128)S(1)}, f32[1,1,8,128]{3,2,1,0:T(8,128)S(1)}, u32[]{:S(2)}, u32[]{:S(2)}) collective-permute-start(f32[1,1,8,128]{3,2,1,0:T(8,128)S(1)} %get-tuple-element.112), channel_id=1, source_target_pairs={{0,32},{32,64},{64,96},{96,128},{128,160},{160,192},{192,224},{224... | collective-permute-start | bytes 12296 | tf_op jit(solution)/shard_map/ppermute | solution.py:24
  63.2 114.0 %collective-permute-start.12 = (f32[1,1,8,128]{3,2,1,0:T(8,128)S(1)}, f32[1,1,8,128]{3,2,1,0:T(8,128)S(1)}, u32[]{:S(2)}, u32[]{:S(2)}) collective-permute-start(f32[1,1,8,128]{3,2,1,0:T(8,128)S(1)} %get-tuple-element.111), channel_id=1, source_target_pairs={{32,0},{64,32},{96,64},{128,96},{160,128},{192,160},{224,192},{256... | collective-permute-start | bytes 12296 | tf_op jit(solution)/shard_map/ppermute | solution.py:25
  78.2 99.0 %collective-permute-start.14 = (f32[1,2,1,128]{3,2,1,0:T(1,128)S(1)}, f32[1,2,1,128]{3,2,1,0:T(1,128)S(1)}, u32[]{:S(2)}, u32[]{:S(2)}) collective-permute-start(f32[1,2,1,128]{3,2,1,0:T(1,128)S(1)} %get-tuple-element.116), channel_id=1, source_target_pairs={{8,0},{16,8},{24,16},{9,1},{17,9},{25,17},{10,2},{18,10},{26,18},{... | collective-permute-start | bytes 3080 | tf_op jit(solution)/shard_map/ppermute | solution.py:39
  79.5 97.7 %collective-permute-start.15 = (f32[1,2,1,128]{3,2,1,0:T(1,128)S(1)}, f32[1,2,1,128]{3,2,1,0:T(1,128)S(1)}, u32[]{:S(2)}, u32[]{:S(2)}) collective-permute-start(f32[1,2,1,128]{3,2,1,0:T(1,128)S(1)} %get-tuple-element.115), channel_id=1, source_target_pairs={{0,8},{8,16},{16,24},{1,9},{9,17},{17,25},{2,10},{10,18},{18,26},{... | collective-permute-start | bytes 3080 | tf_op jit(solution)/shard_map/ppermute | solution.py:38
  83.8 88.8 %collective-permute-start.17 = (f32[1,2,8,1]{3,2,1,0:T(8,128)S(1)}, f32[1,2,8,1]{3,2,1,0:T(8,128)S(1)}, u32[]{:S(2)}, u32[]{:S(2)}) collective-permute-start(f32[1,2,8,1]{3,2,1,0:T(8,128)S(1)} %get-tuple-element.114), channel_id=1, source_target_pairs={{0,1},{1,2},{2,3},{3,4},{4,5},{5,6},{6,7},{8,9},{9,10},{10,11},{11... | collective-permute-start | bytes 200 | tf_op jit(solution)/shard_map/ppermute | solution.py:38
  172.5 4.7 %collective-permute-start.16 = (f32[1,2,8,1]{3,2,1,0:T(8,128)S(1)}, f32[1,2,8,1]{3,2,1,0:T(8,128)S(1)}, u32[]{:S(2)}, u32[]{:S(2)}) collective-permute-start(f32[1,2,8,1]{3,2,1,0:T(8,128)S(1)} %get-tuple-element.113), channel_id=1, source_target_pairs={{1,0},{2,1},{3,2},{4,3},{5,4},{6,5},{7,6},{9,8},{10,9},{11,10},{12... | collective-permute-start | bytes 200 | tf_op jit(solution)/shard_map/ppermute | solution.py:39
  178.1 104.3 %collective-permute-start.19 = (f32[1,1,8,128]{3,2,1,0:T(8,128)S(1)}, f32[1,1,8,128]{3,2,1,0:T(8,128)S(1)}, u32[]{:S(2)}, u32[]{:S(2)}) collective-permute-start(f32[1,1,8,128]{3,2,1,0:T(8,128)S(1)} %get-tuple-element.106), channel_id=1, source_target_pairs={{0,32},{32,64},{64,96},{96,128},{128,160},{160,192},{192,224},{224... | collective-permute-start | bytes 12296 | tf_op jit(solution)/shard_map/ppermute | solution.py:24
  188.5 93.8 %collective-permute-start.18 = (f32[1,1,8,128]{3,2,1,0:T(8,128)S(1)}, f32[1,1,8,128]{3,2,1,0:T(8,128)S(1)}, u32[]{:S(2)}, u32[]{:S(2)}) collective-permute-start(f32[1,1,8,128]{3,2,1,0:T(8,128)S(1)} %get-tuple-element.105), channel_id=1, source_target_pairs={{32,0},{64,32},{96,64},{128,96},{160,128},{192,160},{224,192},{256... | collective-permute-start | bytes 12296 | tf_op jit(solution)/shard_map/ppermute | solution.py:25
  190.5 91.9 %collective-permute-start.20 = (f32[1,2,1,128]{3,2,1,0:T(1,128)S(1)}, f32[1,2,1,128]{3,2,1,0:T(1,128)S(1)}, u32[]{:S(2)}, u32[]{:S(2)}) collective-permute-start(f32[1,2,1,128]{3,2,1,0:T(1,128)S(1)} %get-tuple-element.110), channel_id=1, source_target_pairs={{8,0},{16,8},{24,16},{9,1},{17,9},{25,17},{10,2},{18,10},{26,18},{... | collective-permute-start | bytes 3080 | tf_op jit(solution)/shard_map/ppermute | solution.py:39
  191.8 90.6 %collective-permute-start.21 = (f32[1,2,1,128]{3,2,1,0:T(1,128)S(1)}, f32[1,2,1,128]{3,2,1,0:T(1,128)S(1)}, u32[]{:S(2)}, u32[]{:S(2)}) collective-permute-start(f32[1,2,1,128]{3,2,1,0:T(1,128)S(1)} %get-tuple-element.109), channel_id=1, source_target_pairs={{0,8},{8,16},{16,24},{1,9},{9,17},{17,25},{2,10},{10,18},{18,26},{... | collective-permute-start | bytes 3080 | tf_op jit(solution)/shard_map/ppermute | solution.py:38
  273.6 4.1 collective-permute-start.23
  277.7 4.6 collective-permute-start.22
  283.1 103.0 %collective-permute-start.25 = (f32[1,1,8,128]{3,2,1,0:T(8,128)S(1)}, f32[1,1,8,128]{3,2,1,0:T(8,128)S(1)}, u32[]{:S(2)}, u32[]{:S(2)}) collective-permute-start(f32[1,1,8,128]{3,2,1,0:T(8,128)S(1)} %get-tuple-element.100), channel_id=1, source_target_pairs={{0,32},{32,64},{64,96},{96,128},{128,160},{160,192},{192,224},{224... | collective-permute-start | bytes 12296 | tf_op jit(solution)/shard_map/ppermute | solution.py:24
  294.8 91.3 %collective-permute-start.24 = (f32[1,1,8,128]{3,2,1,0:T(8,128)S(1)}, f32[1,1,8,128]{3,2,1,0:T(8,128)S(1)}, u32[]{:S(2)}, u32[]{:S(2)}) collective-permute-start(f32[1,1,8,128]{3,2,1,0:T(8,128)S(1)} %get-tuple-element.99), channel_id=1, source_target_pairs={{32,0},{64,32},{96,64},{128,96},{160,128},{192,160},{224,192},{256... | collective-permute-start | bytes 12296 | tf_op jit(solution)/shard_map/ppermute | solution.py:25
  296.7 89.3 %collective-permute-start.26 = (f32[1,2,1,128]{3,2,1,0:T(1,128)S(1)}, f32[1,2,1,128]{3,2,1,0:T(1,128)S(1)}, u32[]{:S(2)}, u32[]{:S(2)}) collective-permute-start(f32[1,2,1,128]{3,2,1,0:T(1,128)S(1)} %get-tuple-element.104), channel_id=1, source_target_pairs={{8,0},{16,8},{24,16},{9,1},{17,9},{25,17},{10,2},{18,10},{26,18},{... | collective-permute-start | bytes 3080 | tf_op jit(solution)/shard_map/ppermute | solution.py:39
  298.0 88.0 %collective-permute-start.27 = (f32[1,2,1,128]{3,2,1,0:T(1,128)S(1)}, f32[1,2,1,128]{3,2,1,0:T(1,128)S(1)}, u32[]{:S(2)}, u32[]{:S(2)}) collective-permute-start(f32[1,2,1,128]{3,2,1,0:T(1,128)S(1)} %get-tuple-element.103), channel_id=1, source_target_pairs={{0,8},{8,16},{16,24},{1,9},{9,17},{17,25},{2,10},{10,18},{18,26},{... | collective-permute-start | bytes 3080 | tf_op jit(solution)/shard_map/ppermute | solution.py:38
  379.4 2.1 collective-permute-start.29
  381.4 4.6 collective-permute-start.28
where the time goes:
time: 472 us; the launch traced here: 466 us
  blocking collectives  308 us (65%)
  starting transfers between devices  125 us (26%)
  between operations  15.4 us (3%)
  waiting for transfers between devices  8.55 us (2%)
  other arithmetic  8.01 us (2%)
    psum x20, blocking collectives, by_axis(): return functools.reduce(lax.psum, axes, shard)  308 us
    ppermute x5, starting transfers between devices, extended(): after = lax.ppermute(leading, axis, down)  43.6 us
    ppermute x10, starting transfers between devices, padded(): lax.ppermute(last, axis, up)  37.7 us
    ppermute x5, starting transfers between devices, extended(): before = lax.ppermute(last, axis, up)  30.3 us
    ppermute x10, starting transfers between devices, padded(): lax.ppermute(leading, axis, [(b, a) for a, b in up])  12.9 us
  transfers between devices with their start and end apart: 30, of which 7 were waited for; matrix products, arithmetic and copies ran while one was open for 0% of the time, Pallas kernels for 0%

commit v1 on v0

v1 whole, which is shorter than its diff:
```python
import functools

import jax
import jax.numpy as jnp
from jax import lax
from jax.experimental import pallas as pl
from jax.experimental.pallas import tpu as pltpu
from jax.sharding import PartitionSpec as P

ITERS = 4
TERMS = 6
REGIONS = 4
SHIFTS = (1.0, 25.0, 25.0, 1.0)
PAIRS = tuple((i, j) for i in range(4) for j in range(i, 5))
F32 = jnp.float32


def deviator(grad):
    xx, yy, zz = grad[0][0], grad[1][1], grad[2][2]
    third = (xx + yy + zz) * (1.0 / 3.0)
    return (
        xx - third,
        yy - third,
        zz - third,
        0.5 * (grad[2][1] + grad[1][2]),
        0.5 * (grad[2][0] + grad[0][2]),
        0.5 * (grad[1][0] + grad[0][1]),
    )


def coefficients(gram):
    def form(left, right):
        total = None
        for i, a in enumerate(left):
            row = None
            for j, b in enumerate(right):
                term = b * gram[(min(i, j), max(i, j))]
                row = term if row is None else row + term
            row = a * row
            total = row if total is None else total + row
        return total

    one = jnp.ones_like(gram[(0, 0)])
    res, direction, field = [one], [one], []
    norm = gram[(0, 0)]
    for step in range(ITERS):
        image = []
        for k in range(step + 2):
            value = None
            if k <= step:
                value = SHIFTS[k] * direction[k]
            if k >= 1:
                value = 24.0 * direction[k - 1] if value is None else value + 24.0 * direction[k - 1]
            image.append(value)
        alpha = norm / form(direction, image)
        field = [field[k] + alpha * direction[k] if k < step else alpha * direction[k] for k in range(step + 1)]
        res = [res[k] - alpha * image[k] if k <= step else -alpha * image[k] for k in range(step + 2)]
        if step + 1 < ITERS:
            new = form(res, res)
            beta = new / norm
            direction = [res[k] + beta * direction[k] if k <= step else res[k] for k in range(step + 2)]
            norm = new
    return field, res


def kernel(sizes, *refs):
    nx, ny, nz, zhi = sizes
    low_n = nx // zhi
    line_n = zhi * nz
    plane_n = low_n * ny
    (disp_h, dold_h, visc_h, emax_h, reg_h, dir_h, moduli, times, shear, ratio, scale,
     stress_h, vnext_h, enext_h, field_h, resid_h,
     disp, dold, visc, emax, reg, dirm, stress, vnext, enext, field, resid,
     u, xr, ys, yr, zs, zr, e, eys, eyr, ezs, ezr, gs, gp, ts, tr,
     ld_sem, st_sem, ss, rs, ps_sem, pr_sem, ls_sem, lr_sem, dbl) = refs

    ix, iy, iz = lax.axis_index("gx"), lax.axis_index("gy"), lax.axis_index("gz")
    low, hi = ix % low_n, ix // low_n
    spot = hi * nz + iz
    place = low * ny + iy

    def on_x(d):
        return {"gx": (ix + d + nx) % nx, "gy": iy, "gz": iz}

    def on_y(d):
        return {"gx": ix, "gy": (iy + d + ny) % ny, "gz": iz}

    def on_line(d):
        q = (spot + d + line_n) % line_n
        return {"gx": (q // nz) * low_n + low, "gy": iy, "gz": q % nz}

    def on_plane(d):
        q = (place + d) % plane_n
        return {"gx": hi * low_n + q // ny, "gy": q % ny, "gz": iz}

    def signal(sem, dev):
        pl.semaphore_signal(sem, inc=1, device_id=dev, device_id_type=pl.DeviceIdType.MESH)

    def remote(src, dst, ssem, rsem, dev):
        return pltpu.make_async_remote_copy(
            src_ref=src, dst_ref=dst, send_sem=ssem, recv_sem=rsem,
            device_id=dev, device_id_type=pl.DeviceIdType.MESH)

    loads = [pltpu.make_async_copy(a, b, ld_sem.at[i]) for i, (a, b) in enumerate(
        ((dir_h, dirm), (disp_h, disp), (dold_h, dold), (reg_h, reg), (emax_h, emax), (visc_h, visc)))]
    for c in loads:
        c.start()

    barrier = pltpu.get_barrier_semaphore()
    greet = [on_x(2), on_x(-2), on_x(1), on_x(-1), on_line(1), on_line(-1)]
    greet += [on_plane(d) for d in range(1, plane_n)]
    for dev in greet:
        signal(barrier, dev)

    row = lax.broadcasted_iota(jnp.int32, (8, 128), 0)
    lane = lax.broadcasted_iota(jnp.int32, (8, 128), 1)
    ylo_on = jnp.where(iy > 0, 1.0, 0.0).astype(F32)
    yhi_on = jnp.where(iy < ny - 1, 1.0, 0.0).astype(F32)
    zlo_on = jnp.where(iz > 0, 1.0, 0.0).astype(F32)
    zhi_on = jnp.where(iz < nz - 1, 1.0, 0.0).astype(F32)

    loads[0].wait()
    loads[1].wait()
    loads[2].wait()
    zero = jnp.zeros((8, 128), F32)
    to_hi, to_lo = [zero, zero], [zero, zero]
    for half, src in enumerate((disp, dold)):
        for l in range(2):
            free = (1 - dirm[l]).astype(F32)
            for c in range(3):
                j = l * 3 + c
                val = src[c, l] * free
                u[half, l, c] = val
                ys[half, 0, j] = val[7:8]
                ys[half, 1, j] = val[0:1]
                to_hi[half] = jnp.where(lane == j, pltpu.roll(val, (j - 127) % 128, 1), to_hi[half])
                to_lo[half] = jnp.where(lane == j, pltpu.roll(val, j, 1) if j else val, to_lo[half])
        zs[half, 0] = to_hi[half]
        zs[half, 1] = to_lo[half]

    pl.semaphore_wait(barrier, len(greet))

    faces = []
    for half in range(2):
        faces.append([
            remote(u.at[half, 1], xr.at[half, 0], ss.at[half, 0], rs.at[half, 0], on_x(1)),
            remote(u.at[half, 0], xr.at[half, 1], ss.at[half, 1], rs.at[half, 1], on_x(-1)),
            remote(ys.at[half, 0], yr.at[half, 0], ss.at[half, 2], rs.at[half, 2], on_y(1)),
            remote(ys.at[half, 1], yr.at[half, 1], ss.at[half, 3], rs.at[half, 3], on_y(-1)),
            remote(zs.at[half, 0], zr.at[half, 0], ss.at[half, 4], rs.at[half, 4], on_line(1)),
            remote(zs.at[half, 1], zr.at[half, 1], ss.at[half, 5], rs.at[half, 5], on_line(-1)),
        ])
        for c in faces[half]:
            c.start()

    steps = []
    reach = 1
    while reach < line_n // 2:
        steps.append(reach)
        reach *= 2

    def dbl_signal(s):
        if s < len(steps):
            signal(dbl.at[s], on_line(steps[s]))
            signal(dbl.at[s], on_line(-steps[s]))

    def dbl_wait(s):
        if s < len(steps):
            pl.semaphore_wait(dbl.at[s], 2)

    dbl_signal(0)
    for s in range(len(steps) - 1):
        dbl_wait(s)
        dbl_signal(s + 1)

    loads[3].wait()
    loads[4].wait()

    def pick(table, where_is):
        out = table[REGIONS - 1]
        for k in range(REGIONS - 2, -1, -1):
            out = jnp.where(where_is[k], table[k], out)
        return out

    is_region = [[reg[l] == k for k in range(REGIONS)] for l in range(2)]
    shear_c = [pick([shear[k] for k in range(REGIONS)], is_region[l]) for l in range(2)]
    ratio_c = [pick([ratio[k] for k in range(REGIONS)], is_region[l]) for l in range(2)]
    scale_c = [pick([scale[k] for k in range(REGIONS)], is_region[l]) for l in range(2)]

    def strains(half):
        from_lo = zr[half, 0] * zlo_on
        from_hi = zr[half, 1] * zhi_on
        out = []
        for l in range(2):
            grad = [[None] * 3 for _ in range(3)]
            for c in range(3):
                j = l * 3 + c
                val = u[half, l, c]
                prev_x = xr[half, 0, c] if l == 0 else u[half, 0, c]
                next_x = xr[half, 1, c] if l == 1 else u[half, 1, c]
                below = jnp.broadcast_to(yr[half, 0, j] * ylo_on, (8, 128))
                above = jnp.broadcast_to(yr[half, 1, j] * yhi_on, (8, 128))
                prev_y = pltpu.roll(jnp.where(row == 7, below, val), 1, 0)
                next_y = pltpu.roll(jnp.where(row == 0, above, val), 7, 0)
                prev_z = jnp.where(lane == 0, pltpu.roll(from_lo, (128 - j) % 128, 1), pltpu.roll(val, 1, 1))
                next_z = jnp.where(lane == 127, pltpu.roll(from_hi, 127 - j, 1), pltpu.roll(val, 127, 1))
                grad[0][c] = 0.5 * (next_x - prev_x)
                grad[1][c] = 0.5 * (next_y - prev_y)
                grad[2][c] = 0.5 * (next_z - prev_z)
            out.append(deviator(grad))
        return out

    for c in faces[0]:
        c.wait_recv()
    dev_new = strains(0)
    softening = []
    for l in range(2):
        d = dev_new[l]
        energy = shear_c[l] * (
            d[0] * d[0] + d[1] * d[1] + d[2] * d[2] + 2.0 * (d[3] * d[3] + d[4] * d[4] + d[5] * d[5]))
        peak = jnp.maximum(emax[l], energy)
        soft = 1.0 - lax.erf((peak - energy) / scale_c[l]) / ratio_c[l]
        enext[l] = peak
        softening.append(soft)
        e[4 + l] = soft * energy

    own = e.at[pl.ds(4, 2)]
    wide = [
        remote(own, e.at[pl.ds(2, 2)], ss.at[2, 0], rs.at[2, 0], on_x(1)),
        remote(own, e.at[pl.ds(6, 2)], ss.at[2, 1], rs.at[2, 1], on_x(-1)),
        remote(own, e.at[pl.ds(0, 2)], ss.at[2, 2], rs.at[2, 2], on_x(2)),
        remote(own, e.at[pl.ds(8, 2)], ss.at[2, 3], rs.at[2, 3], on_x(-2)),
    ]
    for c in wide:
        c.start()

    for c in faces[1]:
        c.wait_recv()
    loads[5].wait()
    dev_old = strains(1)
    jump = [[2.0 * shear_c[l] * (dev_new[l][a] - dev_old[l][a]) for a in range(6)] for l in range(2)]
    total = [[None] * 6 for _ in range(2)]
    for k in range(TERMS):
        for l in range(2):
            tau = pick([times[r, k] for r in range(REGIONS)], is_region[l])
            mod = pick([moduli[r, k] for r in range(REGIONS)], is_region[l])
            decay = jnp.exp(-1.0 / tau)
            weight = mod * (1.0 - decay) * tau
            for a in range(6):
                val = decay * visc[k, a, l] + weight * jump[l][a]
                vnext[k, a, l] = val
                total[l][a] = val if k == 0 else total[l][a] + val
    for l in range(2):
        sums = []
        for r in range(REGIONS):
            s = moduli[r, 0]
            for k in range(1, TERMS):
                s = s + moduli[r, k]
            sums.append(1.0 - s)
        factor = pick(sums, is_region[l]) * 2.0 * shear_c[l]
        for a in range(6):
            stress[a, l] = softening[l] * (factor * dev_new[l][a] + total[l][a])
    stores = [pltpu.make_async_copy(a, b, st_sem.at[i]) for i, (a, b) in enumerate(
        ((vnext, vnext_h), (stress, stress_h), (enext, enext_h), (field, field_h), (resid, resid_h)))]
    for c in stores[:3]:
        c.start()

    for c in wide:
        c.wait_recv()
    for l in range(8):
        eys[0, l] = e[1 + l, 4:8]
        eys[1, l] = e[1 + l, 0:4]
    rows = [
        remote(eys.at[0], eyr.at[0], ss.at[3, 0], rs.at[3, 0], on_y(1)),
        remote(eys.at[1], eyr.at[1], ss.at[3, 1], rs.at[3, 1], on_y(-1)),
    ]
    for c in rows:
        c.start()
    row_mask = jnp.where(row < 4, yhi_on, ylo_on)
    lane_mask = jnp.where(lane < 4, zhi_on, jnp.where(lane >= 124, zlo_on, 0.0))
    masks = {(1, 0): row_mask, (0, 1): lane_mask, (1, 1): row_mask * lane_mask}
    to_hi, to_lo = zero, zero

    def pack(val, j, to_hi, to_lo):
        here = (lane >= 4 * j) & (lane < 4 * j + 4)
        to_hi = jnp.where(here, pltpu.roll(val, (4 * j - 124) % 128, 1), to_hi)
        to_lo = jnp.where(here, pltpu.roll(val, 4 * j, 1) if j else val, to_lo)
        return to_hi, to_lo

    basis = {}
    for l in range(10):
        basis[(l, 0, 0)] = e[l]
        if 1 <= l <= 8:
            to_hi, to_lo = pack(basis[(l, 0, 0)], (l - 1) * 2, to_hi, to_lo)
    for c in rows:
        c.wait_recv()
    for l in range(1, 9):
        val = jnp.concatenate([eyr[1, l - 1], eyr[0, l - 1]], axis=0) * row_mask
        basis[(l, 1, 0)] = val
        to_hi, to_lo = pack(val, (l - 1) * 2 + 1, to_hi, to_lo)
    ezs[0] = to_hi
    ezs[1] = to_lo
    cols = [
        remote(ezs.at[0], ezr.at[0], ss.at[3, 2], rs.at[3, 2], on_line(1)),
        remote(ezs.at[1], ezr.at[1], ss.at[3, 3], rs.at[3, 3], on_line(-1)),
    ]
    for c in cols:
        c.start()
    for c in cols:
        c.wait_recv()
    from_lo, from_hi = ezr[0], ezr[1]
    for l in range(1, 9):
        for t in range(2):
            j = (l - 1) * 2 + t
            val = jnp.where(lane < 4,
                            pltpu.roll(from_hi, (128 - 4 * j) % 128, 1),
                            pltpu.roll(from_lo, (124 - 4 * j) % 128, 1))
            basis[(l, t, 1)] = val * masks[(t, 1)]

    def grow(now, k):
        cache = {}

        def rolled(key, amount, axis):
            at = (key, amount, axis)
            if at not in cache:
                cache[at] = pltpu.roll(now[key], amount, axis)
            return cache[at]

        out = {}
        for l in range(k + 1, 9 - k):
            inner = k + 2 <= l <= 7 - k
            for ty, tz in ((0, 0), (1, 0), (0, 1), (1, 1)) if inner else ((0, 0),):
                me = (l, ty, tz)
                acc = now[(l - 1, ty, tz)] + now[(l + 1, ty, tz)]
                acc = acc + jnp.where(row == 7, rolled((l, 1 - ty, tz), 7, 0), rolled(me, 7, 0))
                acc = acc + jnp.where(row == 0, rolled((l, 1 - ty, tz), 1, 0), rolled(me, 1, 0))
                acc = acc + jnp.where(lane == 127, rolled((l, ty, 1 - tz), 127, 1), rolled(me, 127, 1))
                acc = acc + jnp.where(lane == 0, rolled((l, ty, 1 - tz), 1, 1), rolled(me, 1, 1))
                acc = acc * (1.0 / 6.0)
                acc = now[me] - acc if SHIFTS[k] == 1.0 else -acc
                if (ty, tz) != (0, 0):
                    acc = acc * masks[(ty, tz)]
                out[me] = acc
        return out

    powers = [basis]
    for k in range(ITERS):
        powers.append(grow(powers[-1], k))
    vecs = [[p[(4, 0, 0)], p[(5, 0, 0)]] for p in powers]

    sums = zero
    for n, (i, j) in enumerate(PAIRS):
        part = vecs[i][0] * vecs[j][0] + vecs[i][1] * vecs[j][1]
        sums = jnp.where(lane == n, jnp.sum(part, axis=1, keepdims=True), sums)
    mine = jnp.sum(sums, axis=0, keepdims=True)

    gs[0] = mine
    sends = []
    for d in range(1, plane_n):
        c = remote(gs.at[0], gp.at[d - 1], ps_sem, pr_sem, on_plane(d))
        c.start()
    every = remote(gp, gp, ps_sem, pr_sem, on_plane(1))
    every.wait_recv()
    acc = mine
    for d in range(plane_n - 1):
        acc = acc + gp[d]
    ts[0] = acc
    dbl_wait(len(steps) - 1)
    order = sorted(range(1, line_n), key=lambda d: -min(d, line_n - d))
    for d in order:
        c = remote(ts.at[0], tr.at[d - 1], ls_sem, lr_sem, on_line(d))
        c.start()
    along = remote(tr, tr, ls_sem, lr_sem, on_line(1))
    along.wait_recv()
    for d in range(line_n - 1):
        acc = acc + tr[d]

    full = jnp.broadcast_to(acc, (8, 128))
    gram = {pair: jnp.broadcast_to(full[:, n:n + 1], (8, 128)) for n, pair in enumerate(PAIRS)}
    on_field, on_resid = coefficients(gram)
    for l in range(2):
        val = on_field[0] * vecs[0][l]
        for k in range(1, ITERS):
            val = val + on_field[k] * vecs[k][l]
        field[l] = val
        val = on_resid[0] * vecs[0][l]
        for k in range(1, ITERS + 1):
            val = val + on_resid[k] * vecs[k][l]
        resid[l] = val
    for c in stores[3:]:
        c.start()
    for group in (faces[0], faces[1], wide, rows, cols):
        for c in group:
            c.wait_send()
    every.wait_send()
    along.wait_send()
    for c in stores:
        c.wait()


def solution(mesh):
    nx, ny, nz = mesh.shape["gx"], mesh.shape["gy"], mesh.shape["gz"]
    zhi = 4 if nx % 32 == 0 else 2
    low_n = nx // zhi
    line_n, plane_n = zhi * nz, low_n * ny

    def on_device(*args):
        hbm = pl.BlockSpec(memory_space=pl.ANY)
        smem = pl.BlockSpec(memory_space=pltpu.SMEM)
        outs = (
            jax.ShapeDtypeStruct((6, 2, 8, 128), F32),
            jax.ShapeDtypeStruct((6, 6, 2, 8, 128), F32),
            jax.ShapeDtypeStruct((2, 8, 128), F32),
            jax.ShapeDtypeStruct((2, 8, 128), F32),
            jax.ShapeDtypeStruct((2, 8, 128), F32),
        )
        vm = pltpu.VMEM
        dma = pltpu.SemaphoreType.DMA
        return pl.pallas_call(
            functools.partial(kernel, (nx, ny, nz, zhi)),
            out_shape=outs,
            in_specs=[hbm] * 6 + [smem] * 5,
            out_specs=[hbm] * 5,
            scratch_shapes=[
                vm((3, 2, 8, 128), F32), vm((3, 2, 8, 128), F32), vm((6, 6, 2, 8, 128), F32),
                vm((2, 8, 128), F32), vm((2, 8, 128), jnp.int32), vm((2, 8, 128), jnp.int32),
                vm((6, 2, 8, 128), F32), vm((6, 6, 2, 8, 128), F32),
                vm((2, 8, 128), F32), vm((2, 8, 128), F32), vm((2, 8, 128), F32),
                vm((2, 2, 3, 8, 128), F32), vm((2, 2, 3, 8, 128), F32),
                vm((2, 2, 6, 1, 128), F32), vm((2, 2, 6, 1, 128), F32),
                vm((2, 2, 8, 128), F32), vm((2, 2, 8, 128), F32),
                vm((10, 8, 128), F32),
                vm((2, 8, 4, 128), F32), vm((2, 8, 4, 128), F32),
                vm((2, 8, 128), F32), vm((2, 8, 128), F32),
                vm((1, 1, 128), F32), vm((plane_n - 1, 1, 128), F32),
                vm((1, 1, 128), F32), vm((line_n - 1, 1, 128), F32),
                dma((6,)), dma((5,)), dma((4, 6)), dma((4, 6)), dma, dma, dma, dma,
                pltpu.SemaphoreType.REGULAR((4,)),
            ],
            compiler_params=pltpu.CompilerParams(collective_id=0, has_side_effects=True),
        )(*args)

    cell = P("gx", "gy", "gz")
    vec = P(None, "gx", "gy", "gz")
    ten = P(None, None, "gx", "gy", "gz")
    return jax.shard_map(
        on_device,
        mesh=mesh,
        in_specs=(vec, vec, ten, cell, cell, cell, P(), P(), P(), P(), P()),
        out_specs=(vec, ten, cell, cell, cell),
        check_vma=False,
    )
```

time: 472 us -> 72 us (0.15); the launches traced: 466 us -> 71.7 us
  blocking collectives: 308 us -> 0 us
  starting transfers between devices: 125 us -> 0 us
  Pallas kernels: 0 us -> 65.9 us
  between operations: 15.4 us -> 0.65 us
  waiting for transfers between devices: 8.55 us -> 0 us
  other arithmetic: 8.01 us -> 0 us
    psum x20 -> x0, blocking collectives: 308 us -> none  [by_axis(): return functools.reduce(lax.psum, axes, shard)]
    ppermute x30 -> x0, starting transfers between devices: 125 us -> none  [the longest x5 43.6 us: extended(): after = lax.ppermute(leading, axis, down)]
    pallas_call x0 -> x1, Pallas kernels: none -> 65.9 us  [on_device(): pl.pallas_call(functools.partial(kernel, (nx, ny, nz, zhi)), out_shape=ou...]
    ppermute x30 -> x0, waiting for transfers between devices: 8.55 us -> none  [the longest x10 7.42 us: padded(): lax.ppermute(leading, axis, [(b, a) for a, b in up])]
    reduce_sum x8 -> x0, other arithmetic: 5.05 us -> none  [the longest x4 2.83 us: on_device(): jnp.sum(image_res * residual)]
  transfers between devices with their start and end apart: 30 -> 0, of which waited for: 7 -> 0; matrix products, arithmetic and copies ran while one was open for 0% -> 0% of each run, Pallas kernels for 0% -> 0%
where the time goes in v1:
time: 72 us; the launch traced here: 71.7 us
  Pallas kernels  65.9 us (92%)
  local copies, waits for them, and re-layouts  5.13 us (7%)
    pallas_call x1, Pallas kernels, on_device(): pl.pallas_call(functools.partial(kernel, (nx, ny, nz, zhi)), out_shape=ou...  65.9 us
    unnamed x11, local copies, waits for them, and re-layouts  5.13 us

profile of v1, /device:TPU:1, one launch (start us, length us, event | category | flops | bytes accessed | tf_op | source)
XLA Modules:
  0.0 71.7 jit_solution(18230864408572614598)
XLA Ops:
  0.6 65.9 %shard_map.146 = (f32[6,2,8,128]{3,2,1,0:T(8,128)}, f32[6,6,2,8,128]{4,3,2,1,0:T(8,128)}, f32[2,8,128]{2,1,0:T(8,128)}, f32[2,8,128]{2,1,0:T(8,128)}, f32[2,8,128]{2,1,0:T(8,128)}) custom-call(f32[3,2,8,128]{3,2,1,0:T(8,128)} %refs_0_.1, f32[3,2,8,128]{3,2,1,0:T(8,128)} %refs_1_.1, f32[6,6,2,8,128]{4,3,2,1,0:T(8,128)} %refs_2_.1, f32[2,8,128]{2,1,0:T(8,128)} %refs_3_.1, ...), custom_call_target="tpu_custom_call" | custom-call | tf_op jit(solution)/shard_map/pallas_call | solution.py:419
  66.6 1.4 %copy.21 = f32[6,2,8,128]{3,2,1,0:T(8,128)} copy(f32[6,2,8,128]{3,2,1,0:T(8,128)} %get-tuple-element.10) | data formatting | bytes 98304
  68.0 0.0 copy-start.2
  68.0 1.7 %copy.22 = f32[6,6,2,8,128]{4,3,2,1,0:T(8,128)} copy(f32[6,6,2,8,128]{4,3,2,1,0:T(8,128)} %get-tuple-element.11) | data formatting | bytes 589824
  69.7 0.0 copy-done.2
  69.7 0.0 copy-start.1
  69.7 0.6 copy.23
  70.3 0.1 copy-done.1
  70.4 0.0 copy-start
  70.4 0.6 copy.24
  71.0 0.1 copy-done
  71.1 0.6 copy.25
Async XLA Ops:
  68.0 1.7 %copy-start.2 = (f32[2,8,128]{2,1,0:T(8,128)S(1)}, f32[2,8,128]{2,1,0:T(8,128)}, u32[]{:S(2)}) copy-start(f32[2,8,128]{2,1,0:T(8,128)} %get-tuple-element.12) | copy-start | bytes 24580
  69.7 0.7 copy-start.1
  70.4 0.7 copy-start

commit v2 on v1

v2 whole, which is shorter than its diff:
```python
import functools

import jax
import jax.numpy as jnp
from jax import lax
from jax.experimental import pallas as pl
from jax.experimental.pallas import tpu as pltpu
from jax.sharding import PartitionSpec as P

ITERS = 4
TERMS = 6
REGIONS = 4
SHIFTS = (1.0, 25.0, 25.0, 1.0)
PAIRS = tuple((i, j) for i in range(4) for j in range(i, 5))
F32 = jnp.float32


def deviator(grad):
    xx, yy, zz = grad[0][0], grad[1][1], grad[2][2]
    third = (xx + yy + zz) * (1.0 / 3.0)
    return (
        xx - third,
        yy - third,
        zz - third,
        0.5 * (grad[2][1] + grad[1][2]),
        0.5 * (grad[2][0] + grad[0][2]),
        0.5 * (grad[1][0] + grad[0][1]),
    )


def coefficients(gram):
    def form(left, right):
        total = None
        for i, a in enumerate(left):
            row = None
            for j, b in enumerate(right):
                term = b * gram[(min(i, j), max(i, j))]
                row = term if row is None else row + term
            row = a * row
            total = row if total is None else total + row
        return total

    one = jnp.ones_like(gram[(0, 0)])
    res, direction, field = [one], [one], []
    norm = gram[(0, 0)]
    for step in range(ITERS):
        image = []
        for k in range(step + 2):
            value = None
            if k <= step:
                value = SHIFTS[k] * direction[k]
            if k >= 1:
                value = 24.0 * direction[k - 1] if value is None else value + 24.0 * direction[k - 1]
            image.append(value)
        alpha = norm / form(direction, image)
        field = [field[k] + alpha * direction[k] if k < step else alpha * direction[k] for k in range(step + 1)]
        res = [res[k] - alpha * image[k] if k <= step else -alpha * image[k] for k in range(step + 2)]
        if step + 1 < ITERS:
            new = form(res, res)
            beta = new / norm
            direction = [res[k] + beta * direction[k] if k <= step else res[k] for k in range(step + 2)]
            norm = new
    return field, res


def kernel(sizes, *refs):
    nx, ny, nz, zhi = sizes
    low_n = nx // zhi
    line_n = zhi * nz
    plane_n = low_n * ny
    half_way = nz // 2
    (disp_h, dold_h, visc_h, emax_h, reg_h, dir_h, moduli_h, times_h, shear_h, ratio_h, scale_h,
     stress, vnext, enext, vout, sums_out,
     disp, dold, visc, emax, reg, dirm, moduli, times, shear, ratio, scale,
     u, xr, ys, yr, zs, zr, e, eys, eyr, ezs, ezr, gs, gp, ts, tr,
     ld_sem, ss, rs, ps_sem, pr_sem, ls_sem, lr_sem, dbl, xok) = refs

    ix, iy, iz = lax.axis_index("gx"), lax.axis_index("gy"), lax.axis_index("gz")
    low, hi = ix % low_n, ix // low_n
    spot = hi * nz + iz
    place = low * ny + iy
    top = low == low_n - 1
    bottom = low == 0

    def on_x(d):
        return {"gx": (ix + d + nx) % nx, "gy": iy, "gz": iz}

    def at(d, low_to, dy=0):
        q = (spot + d + line_n) % line_n
        return {"gx": (q // nz) * low_n + low_to, "gy": (iy + dy + ny) % ny, "gz": q % nz}

    def on_line(d, dy=0):
        return at(d, low, dy)

    def on_plane(d):
        q = (place + d) % plane_n
        return {"gx": hi * low_n + q // ny, "gy": q % ny, "gz": iz}

    def either(cond, one, other):
        return {k: jnp.where(cond, one[k], other[k]) for k in one}

    def signal(sem, dev):
        pl.semaphore_signal(sem, inc=1, device_id=dev, device_id_type=pl.DeviceIdType.MESH)

    def remote(src, dst, ssem, rsem, dev):
        return pltpu.make_async_remote_copy(
            src_ref=src, dst_ref=dst, send_sem=ssem, recv_sem=rsem,
            device_id=dev, device_id_type=pl.DeviceIdType.MESH)

    loads = [pltpu.make_async_copy(a, b, ld_sem.at[i]) for i, (a, b) in enumerate(
        ((dir_h, dirm), (disp_h, disp), (dold_h, dold), (reg_h, reg), (emax_h, emax),
         (shear_h, shear), (ratio_h, ratio), (scale_h, scale), (moduli_h, moduli), (times_h, times),
         (visc_h, visc)))]
    for c in loads[:2]:
        c.start()

    barrier = pltpu.get_barrier_semaphore()
    mirror = low_n - 1 - low
    greet = [at(half_way, mirror), at(-half_way, mirror), on_line(half_way), on_line(-half_way)]
    greet += [on_plane(d) for d in range(1, plane_n)]
    greet += [on_line(1), on_line(-1)]
    for dev in greet:
        signal(barrier, dev)
    for c in loads[2:]:
        c.start()

    row = lax.broadcasted_iota(jnp.int32, (8, 128), 0)
    lane = lax.broadcasted_iota(jnp.int32, (8, 128), 1)
    ylo_on = jnp.where(iy > 0, 1.0, 0.0).astype(F32)
    yhi_on = jnp.where(iy < ny - 1, 1.0, 0.0).astype(F32)
    zlo_on = jnp.where(iz > 0, 1.0, 0.0).astype(F32)
    zhi_on = jnp.where(iz < nz - 1, 1.0, 0.0).astype(F32)

    def hold(half, src):
        to_hi, to_lo = zero, zero
        for l in range(2):
            free = (1 - dirm[l]).astype(F32)
            for c in range(3):
                j = l * 3 + c
                val = src[c, l] * free
                u[half, l, c] = val
                ys[half, 0, j] = val[7:8]
                ys[half, 1, j] = val[0:1]
                to_hi = jnp.where(lane == j, pltpu.roll(val, (j - 127) % 128, 1), to_hi)
                to_lo = jnp.where(lane == j, pltpu.roll(val, j, 1) if j else val, to_lo)
        zs[half, 0] = to_hi
        zs[half, 1] = to_lo

    def send_faces(half):
        out = [
            remote(u.at[half, 1], xr.at[half, jnp.where(top, 2, 0)], ss.at[half, 0],
                   rs.at[half, jnp.where(top, 6, 0)], either(top, on_line(half_way), on_x(1))),
            remote(u.at[half, 0], xr.at[half, jnp.where(bottom, 2, 1)], ss.at[half, 1],
                   rs.at[half, jnp.where(bottom, 6, 1)], either(bottom, on_line(-half_way), on_x(-1))),
            remote(ys.at[half, 0], yr.at[half, 0], ss.at[half, 2], rs.at[half, 2], on_line(0, 1)),
            remote(ys.at[half, 1], yr.at[half, 1], ss.at[half, 3], rs.at[half, 3], on_line(0, -1)),
            remote(zs.at[half, 0], zr.at[half, 0], ss.at[half, 4], rs.at[half, 4], on_line(1)),
            remote(zs.at[half, 1], zr.at[half, 1], ss.at[half, 5], rs.at[half, 5], on_line(-1)),
        ]
        for c in out:
            c.start()
        return out

    def relay(half):
        side = jnp.where(top, 0, 1)
        return remote(xr.at[half, 2], xr.at[half, side], ss.at[half, 6], rs.at[half, side],
                      either(top, at(half_way, 0), at(-half_way, low_n - 1)))

    def pass_on(half):
        @pl.when(top | bottom)
        def _():
            remote(xr.at[half, 2], xr.at[half, 2], ss.at[half, 6], rs.at[half, 6], on_line(1)).wait_recv()
            relay(half).start()

    def wait_faces(half):
        for i, dst in enumerate((xr.at[half, 0], xr.at[half, 1], yr.at[half, 0], yr.at[half, 1],
                                 zr.at[half, 0], zr.at[half, 1])):
            remote(dst, dst, ss.at[half, i], rs.at[half, i], on_line(1)).wait_recv()

    zero = jnp.zeros((8, 128), F32)
    loads[0].wait()
    loads[1].wait()
    hold(0, disp)
    pl.semaphore_wait(barrier, len(greet))
    faces = [send_faces(0)]

    steps = []
    reach = 1
    while reach < line_n // 2:
        steps.append(reach)
        reach *= 2

    def dbl_signal(s):
        if s < len(steps):
            signal(dbl.at[s], on_line(steps[s]))
            signal(dbl.at[s], on_line(-steps[s]))

    known = set()

    def dbl_wait(s):
        if s < len(steps) and s not in known:
            known.add(s)
            pl.semaphore_wait(dbl.at[s], 2)

    dbl_signal(0)
    for c in loads[2:10]:
        c.wait()
    hold(1, dold)
    dbl_wait(0)
    dbl_signal(1)
    pass_on(0)

    def pick(table, where_is):
        out = table[REGIONS - 1]
        for k in range(REGIONS - 2, -1, -1):
            out = jnp.where(where_is[k], table[k], out)
        return out

    is_region = [[reg[l] == k for k in range(REGIONS)] for l in range(2)]
    shear_c = [pick([shear[k] for k in range(REGIONS)], is_region[l]) for l in range(2)]
    ratio_c = [pick([ratio[k] for k in range(REGIONS)], is_region[l]) for l in range(2)]
    scale_c = [pick([scale[k] for k in range(REGIONS)], is_region[l]) for l in range(2)]

    def strains(half):
        from_lo = zr[half, 0] * zlo_on
        from_hi = zr[half, 1] * zhi_on
        out = []
        for l in range(2):
            grad = [[None] * 3 for _ in range(3)]
            for c in range(3):
                j = l * 3 + c
                val = u[half, l, c]
                prev_x = xr[half, 0, c] if l == 0 else u[half, 0, c]
                next_x = xr[half, 1, c] if l == 1 else u[half, 1, c]
                below = jnp.broadcast_to(yr[half, 0, j] * ylo_on, (8, 128))
                above = jnp.broadcast_to(yr[half, 1, j] * yhi_on, (8, 128))
                prev_y = pltpu.roll(jnp.where(row == 7, below, val), 1, 0)
                next_y = pltpu.roll(jnp.where(row == 0, above, val), 7, 0)
                prev_z = jnp.where(lane == 0, pltpu.roll(from_lo, (128 - j) % 128, 1), pltpu.roll(val, 1, 1))
                next_z = jnp.where(lane == 127, pltpu.roll(from_hi, 127 - j, 1), pltpu.roll(val, 127, 1))
                grad[0][c] = 0.5 * (next_x - prev_x)
                grad[1][c] = 0.5 * (next_y - prev_y)
                grad[2][c] = 0.5 * (next_z - prev_z)
            out.append(deviator(grad))
        return out

    wait_faces(0)

    @pl.when(top)
    def _():
        signal(xok, on_x(-1))

    @pl.when(bottom)
    def _():
        signal(xok, on_x(1))

    dev_new = strains(0)
    softening = []
    for l in range(2):
        d = dev_new[l]
        energy = shear_c[l] * (
            d[0] * d[0] + d[1] * d[1] + d[2] * d[2] + 2.0 * (d[3] * d[3] + d[4] * d[4] + d[5] * d[5]))
        peak = jnp.maximum(emax[l], energy)
        soft = 1.0 - lax.erf((peak - energy) / scale_c[l]) / ratio_c[l]
        enext[l] = peak
        softening.append(soft)
        e[4 + l] = soft * energy

    own = e.at[pl.ds(4, 2)]
    wide = [
        remote(own, e.at[pl.ds(2, 2)], ss.at[2, 0], rs.at[2, 0], on_x(1)),
        remote(own, e.at[pl.ds(6, 2)], ss.at[2, 1], rs.at[2, 1], on_x(-1)),
        remote(own, e.at[pl.ds(0, 2)], ss.at[2, 2], rs.at[2, 2], on_x(2)),
        remote(own, e.at[pl.ds(8, 2)], ss.at[2, 3], rs.at[2, 3], on_x(-2)),
    ]
    for c in wide[:2]:
        c.start()

    @pl.when((low == low_n - 2) | (low == 1))
    def _():
        pl.semaphore_wait(xok, 1)

    for c in wide[2:]:
        c.start()
    faces.append(send_faces(1))
    dbl_wait(1)
    dbl_signal(2)
    pass_on(1)
    dbl_wait(2)
    dbl_signal(3)


    row_mask = jnp.where(row < 4, yhi_on, ylo_on)
    lane_mask = jnp.where(lane < 4, zhi_on, jnp.where(lane >= 124, zlo_on, 0.0))
    masks = {(1, 0): row_mask, (0, 1): lane_mask, (1, 1): row_mask * lane_mask}
    to_hi, to_lo = zero, zero
    basis = {}
    for l in (4, 5, 2, 3, 6, 7, 0, 1, 8, 9):
        if l in (2, 6, 0, 8):
            wide[(2, 6, 0, 8).index(l)].wait_recv()
        val = e[l]
        basis[(l, 0, 0)] = val
        if 1 <= l <= 8:
            j = l - 1
            eys[0, j] = val[4:8]
            eys[1, j] = val[0:4]
            here = (lane >= 4 * j) & (lane < 4 * j + 4)
            to_hi = jnp.where(here, pltpu.roll(val, (4 * j - 124) % 128, 1), to_hi)
            to_lo = jnp.where(here, pltpu.roll(val, 4 * j, 1) if j else val, to_lo)
    ezs[0] = to_hi
    ezs[1] = to_lo
    edges = [
        remote(ezs.at[0], ezr.at[2], ss.at[3, 0], rs.at[3, 0], on_line(1, 1)),
        remote(ezs.at[0], ezr.at[3], ss.at[3, 1], rs.at[3, 1], on_line(1, -1)),
        remote(ezs.at[1], ezr.at[4], ss.at[3, 2], rs.at[3, 2], on_line(-1, 1)),
        remote(ezs.at[1], ezr.at[5], ss.at[3, 3], rs.at[3, 3], on_line(-1, -1)),
        remote(ezs.at[0], ezr.at[0], ss.at[3, 4], rs.at[3, 4], on_line(1)),
        remote(ezs.at[1], ezr.at[1], ss.at[3, 5], rs.at[3, 5], on_line(-1)),
        remote(eys.at[0], eyr.at[0], ss.at[3, 6], rs.at[3, 6], on_line(0, 1)),
        remote(eys.at[1], eyr.at[1], ss.at[3, 7], rs.at[3, 7], on_line(0, -1)),
    ]
    for c in edges:
        c.start()
    for c in edges[6:]:
        c.wait_recv()
    for l in range(1, 9):
        basis[(l, 1, 0)] = jnp.concatenate([eyr[1, l - 1], eyr[0, l - 1]], axis=0) * row_mask
    for c in edges[:6]:
        c.wait_recv()
    sides = ((ezr[0], ezr[1]),
             (jnp.where(row < 4, ezr[3], ezr[2]), jnp.where(row < 4, ezr[5], ezr[4])))
    for l in range(1, 9):
        for t in range(2):
            j = l - 1
            from_lo, from_hi = sides[t]
            val = jnp.where(lane < 4,
                            pltpu.roll(from_hi, 128 - 4 * j, 1) if j else from_hi,
                            pltpu.roll(from_lo, 124 - 4 * j, 1))
            basis[(l, t, 1)] = val * masks[(t, 1)]

    def grow(now, k):
        cache = {}

        def rolled(key, amount, axis):
            at = (key, amount, axis)
            if at not in cache:
                cache[at] = pltpu.roll(now[key], amount, axis)
            return cache[at]

        out = {}
        for l in range(k + 1, 9 - k):
            inner = k + 2 <= l <= 7 - k
            for ty, tz in ((0, 0), (1, 0), (0, 1), (1, 1)) if inner else ((0, 0),):
                me = (l, ty, tz)
                acc = now[(l - 1, ty, tz)] + now[(l + 1, ty, tz)]
                acc = acc + jnp.where(row == 7, rolled((l, 1 - ty, tz), 7, 0), rolled(me, 7, 0))
                acc = acc + jnp.where(row == 0, rolled((l, 1 - ty, tz), 1, 0), rolled(me, 1, 0))
                acc = acc + jnp.where(lane == 127, rolled((l, ty, 1 - tz), 127, 1), rolled(me, 127, 1))
                acc = acc + jnp.where(lane == 0, rolled((l, ty, 1 - tz), 1, 1), rolled(me, 1, 1))
                acc = acc * (1.0 / 6.0)
                acc = now[me] - acc if SHIFTS[k] == 1.0 else -acc
                if (ty, tz) != (0, 0):
                    acc = acc * masks[(ty, tz)]
                out[me] = acc
        return out

    powers = [basis]
    for k in range(ITERS):
        powers.append(grow(powers[-1], k))
    vecs = [[p[(4, 0, 0)], p[(5, 0, 0)]] for p in powers]

    for k in range(ITERS + 1):
        for l in range(2):
            vout[2 * k + l] = vecs[k][l]
    sums = zero
    for n, (i, j) in enumerate(PAIRS):
        part = vecs[i][0] * vecs[j][0] + vecs[i][1] * vecs[j][1]
        sums = jnp.where(lane == n, jnp.sum(part, axis=1, keepdims=True), sums)
    mine = jnp.sum(sums, axis=0, keepdims=True)

    gs[0] = mine
    sends = []
    for d in range(1, plane_n):
        c = remote(gs.at[0], gp.at[d - 1], ps_sem, pr_sem, on_plane(d))
        c.start()
    every = remote(gp, gp, ps_sem, pr_sem, on_plane(1))
    every.wait_recv()
    acc = mine
    for d in range(plane_n - 1):
        acc = acc + gp[d]
    ts[0] = acc
    dbl_wait(len(steps) - 1)
    order = sorted(range(1, line_n), key=lambda d: -min(d, line_n - d))
    for d in order:
        c = remote(ts.at[0], tr.at[d - 1], ls_sem, lr_sem, on_line(d))
        c.start()
    wait_faces(1)
    loads[10].wait()
    dev_old = strains(1)
    jump = [[2.0 * shear_c[l] * (dev_new[l][a] - dev_old[l][a]) for a in range(6)] for l in range(2)]
    total = [[None] * 6 for _ in range(2)]
    for k in range(TERMS):
        for l in range(2):
            tau = pick([times[r, k] for r in range(REGIONS)], is_region[l])
            mod = pick([moduli[r, k] for r in range(REGIONS)], is_region[l])
            decay = jnp.exp(-1.0 / tau)
            weight = mod * (1.0 - decay) * tau
            for a in range(6):
                val = decay * visc[k, a, l] + weight * jump[l][a]
                vnext[k, a, l] = val
                total[l][a] = val if k == 0 else total[l][a] + val
    for l in range(2):
        sums = []
        for r in range(REGIONS):
            s = moduli[r, 0]
            for k in range(1, TERMS):
                s = s + moduli[r, k]
            sums.append(1.0 - s)
        factor = pick(sums, is_region[l]) * 2.0 * shear_c[l]
        for a in range(6):
            stress[a, l] = softening[l] * (factor * dev_new[l][a] + total[l][a])

    along = remote(tr, tr, ls_sem, lr_sem, on_line(1))
    along.wait_recv()
    for d in range(line_n - 1):
        acc = acc + tr[d]
    sums_out[...] = acc

    for group in (faces[0], faces[1], wide, edges):
        for c in group:
            c.wait_send()

    @pl.when(top | bottom)
    def _():
        relay(0).wait_send()
        relay(1).wait_send()

    every.wait_send()
    along.wait_send()


def finish(stress, vnext, enext, vecs, sums, stress_h, vnext_h, enext_h, field_h, resid_h, field, resid, sem):
    stores = [pltpu.make_async_copy(a, b, sem.at[i]) for i, (a, b) in enumerate(
        ((vnext, vnext_h), (stress, stress_h), (enext, enext_h), (field, field_h), (resid, resid_h)))]
    for c in stores[:3]:
        c.start()
    full = jnp.broadcast_to(sums[...], (8, 128))
    gram = {pair: jnp.broadcast_to(full[:, n:n + 1], (8, 128)) for n, pair in enumerate(PAIRS)}
    on_field, on_resid = coefficients(gram)
    for l in range(2):
        val = on_field[0] * vecs[l]
        for k in range(1, ITERS):
            val = val + on_field[k] * vecs[2 * k + l]
        field[l] = val
        val = on_resid[0] * vecs[l]
        for k in range(1, ITERS + 1):
            val = val + on_resid[k] * vecs[2 * k + l]
        resid[l] = val
    for c in stores[3:]:
        c.start()
    for c in stores:
        c.wait()


def solution(mesh):
    nx, ny, nz = mesh.shape["gx"], mesh.shape["gy"], mesh.shape["gz"]
    zhi = 4 if nx % 32 == 0 else 2
    low_n = nx // zhi
    line_n, plane_n = zhi * nz, low_n * ny

    def on_device(*args):
        hbm = pl.BlockSpec(memory_space=pltpu.HBM)
        local = pl.BlockSpec(memory_space=pltpu.VMEM)
        vm = pltpu.VMEM
        sm = pltpu.SMEM
        dma = pltpu.SemaphoreType.DMA
        cells = jax.ShapeDtypeStruct((2, 8, 128), F32)
        stress = jax.ShapeDtypeStruct((6, 2, 8, 128), F32)
        visco = jax.ShapeDtypeStruct((6, 6, 2, 8, 128), F32)
        parts = pl.pallas_call(
            functools.partial(kernel, (nx, ny, nz, zhi)),
            out_shape=(stress, visco, cells,
                       jax.ShapeDtypeStruct((10, 8, 128), F32), jax.ShapeDtypeStruct((1, 128), F32)),
            in_specs=[hbm] * 11,
            out_specs=[local] * 5,
            scratch_shapes=[
                vm((3, 2, 8, 128), F32), vm((3, 2, 8, 128), F32), vm((6, 6, 2, 8, 128), F32),
                vm((2, 8, 128), F32), vm((2, 8, 128), jnp.int32), vm((2, 8, 128), jnp.int32),
                sm((4, 6), F32), sm((4, 6), F32), sm((4,), F32), sm((4,), F32), sm((4,), F32),
                vm((2, 2, 3, 8, 128), F32), vm((2, 3, 3, 8, 128), F32),
                vm((2, 2, 6, 1, 128), F32), vm((2, 2, 6, 1, 128), F32),
                vm((2, 2, 8, 128), F32), vm((2, 2, 8, 128), F32),
                vm((10, 8, 128), F32),
                vm((2, 8, 4, 128), F32), vm((2, 8, 4, 128), F32),
                vm((2, 8, 128), F32), vm((6, 8, 128), F32),
                vm((1, 1, 128), F32), vm((plane_n - 1, 1, 128), F32),
                vm((1, 1, 128), F32), vm((line_n - 1, 1, 128), F32),
                dma((11,)), dma((4, 8)), dma((4, 8)), dma, dma, dma, dma,
                pltpu.SemaphoreType.REGULAR((4,)), pltpu.SemaphoreType.REGULAR,
            ],
            compiler_params=pltpu.CompilerParams(
                collective_id=0, has_side_effects=True, vmem_limit_bytes=16 << 20),
        )(*[pltpu.with_memory_space_constraint(a, pltpu.HBM) for a in args])
        return pl.pallas_call(
            finish,
            out_shape=(stress, visco, cells, cells, cells),
            in_specs=[local] * 5,
            out_specs=[hbm] * 5,
            scratch_shapes=[vm((2, 8, 128), F32), vm((2, 8, 128), F32), dma((5,))],
            compiler_params=pltpu.CompilerParams(vmem_limit_bytes=16 << 20),
        )(*parts)

    cell = P("gx", "gy", "gz")
    vec = P(None, "gx", "gy", "gz")
    ten = P(None, None, "gx", "gy", "gz")
    return jax.shard_map(
        on_device,
        mesh=mesh,
        in_specs=(vec, vec, ten, cell, cell, cell, P(), P(), P(), P(), P()),
        out_specs=(vec, ten, cell, cell, cell),
        check_vma=False,
    )
```

time: 72 us -> 65.1 us (0.904)
  local copies, waits for them, and re-layouts: 5.13 us -> 0 us
  Pallas kernels: 65.9 us -> 64.2 us
    unnamed x11 -> x0, local copies, waits for them, and re-layouts: 5.13 us -> none
    pallas_call x1 -> x2, Pallas kernels: 65.9 us -> 64.2 us  [the longest x1 63.4 us: on_device(): pl.pallas_call(functools.partial(kernel, (nx, ny, nz, zhi)), out_shape=(s...]
where the time goes in v2:
time: 65.1 us; the launch traced here: 64.9 us
  Pallas kernels  64.2 us (99%)
    pallas_call x1, Pallas kernels, on_device(): pl.pallas_call(functools.partial(kernel, (nx, ny, nz, zhi)), out_shape=(s...  63.4 us

profile of v2, /device:TPU:1, one launch (start us, length us, event | category | flops | bytes accessed | tf_op | source)
XLA Modules:
  0.0 64.9 jit_solution(14252255683840444508)
XLA Ops:
  0.6 63.4 %shard_map.146 = (f32[6,2,8,128]{3,2,1,0:T(8,128)S(1)}, f32[6,6,2,8,128]{4,3,2,1,0:T(8,128)S(1)}, f32[2,8,128]{2,1,0:T(8,128)S(1)}, f32[10,8,128]{2,1,0:T(8,128)S(1)}, f32[1,128]{1,0:T(1,128)S(1)}) custom-call(f32[3,2,8,128]{3,2,1,0:T(8,128)} %refs_0_.1, f32[3,2,8,128]{3,2,1,0:T(8,128)} %refs_1_.1, f32[6,6,2,8,128]{4,3,2,1,0:T(8,128)} %refs_2_.1, ...), custom_call_target="tpu_custom_call" | custom-call | tf_op jit(solution)/shard_map/pallas_call | solution.py:480
  64.1 0.8 %shard_map.147 = (f32[6,2,8,128]{3,2,1,0:T(8,128)}, f32[6,6,2,8,128]{4,3,2,1,0:T(8,128)}, f32[2,8,128]{2,1,0:T(8,128)}, f32[2,8,128]{2,1,0:T(8,128)}, f32[2,8,128]{2,1,0:T(8,128)}) custom-call(f32[6,2,8,128]{3,2,1,0:T(8,128)S(1)} %get-tuple-element.10.stress, f32[6,6,2,8,128]{4,3,2,1,0:T(8,128)S(1)} %get-tuple-element.11.vnext, ...), custom_call_target="tpu_custom_call" | custom-call | tf_op jit(solution)/shard_map/pallas_call | solution.py:504

commit v3 on v2

--- a/solution.py
+++ b/solution.py
@@ -15,16 +15,20 @@
 F32 = jnp.float32
 
 
-def deviator(grad):
-    xx, yy, zz = grad[0][0], grad[1][1], grad[2][2]
+def flat_parts(grad_y, grad_z):
+    return (grad_y[1], grad_z[2], 0.5 * (grad_z[1] + grad_y[2]), grad_z[0], grad_y[0])
+
+
+def deviator(grad_x, flat):
+    xx, yy, zz = grad_x[0], flat[0], flat[1]
     third = (xx + yy + zz) * (1.0 / 3.0)
     return (
         xx - third,
         yy - third,
         zz - third,
-        0.5 * (grad[2][1] + grad[1][2]),
-        0.5 * (grad[2][0] + grad[0][2]),
-        0.5 * (grad[1][0] + grad[0][1]),
+        flat[2],
+        0.5 * (flat[3] + grad_x[2]),
+        0.5 * (flat[4] + grad_x[1]),
     )
 
 
@@ -73,7 +77,7 @@
      stress, vnext, enext, vout, sums_out,
      disp, dold, visc, emax, reg, dirm, moduli, times, shear, ratio, scale,
      u, xr, ys, yr, zs, zr, e, eys, eyr, ezs, ezr, gs, gp, ts, tr,
-     ld_sem, ss, rs, ps_sem, pr_sem, ls_sem, lr_sem, dbl, xok) = refs
+     pk, mk, mu, ld_sem, ss, rs, ps_sem, pr_sem, ls_sem, lr_sem, dbl) = refs
 
     ix, iy, iz = lax.axis_index("gx"), lax.axis_index("gy"), lax.axis_index("gz")
     low, hi = ix % low_n, ix // low_n
@@ -115,8 +119,7 @@
         c.start()
 
     barrier = pltpu.get_barrier_semaphore()
-    mirror = low_n - 1 - low
-    greet = [at(half_way, mirror), at(-half_way, mirror), on_line(half_way), on_line(-half_way)]
+    greet = [at(s, (low + r + low_n) % low_n) for r in (0, 1, -1, 2, -2) for s in (half_way, -half_way)]
     greet += [on_plane(d) for d in range(1, plane_n)]
     greet += [on_line(1), on_line(-1)]
     for dev in greet:
@@ -172,17 +175,53 @@
             remote(xr.at[half, 2], xr.at[half, 2], ss.at[half, 6], rs.at[half, 6], on_line(1)).wait_recv()
             relay(half).start()
 
-    def wait_faces(half):
-        for i, dst in enumerate((xr.at[half, 0], xr.at[half, 1], yr.at[half, 0], yr.at[half, 1],
-                                 zr.at[half, 0], zr.at[half, 1])):
-            remote(dst, dst, ss.at[half, i], rs.at[half, i], on_line(1)).wait_recv()
+    def wait_face(half, i):
+        dst = (xr.at[half, 0], xr.at[half, 1], yr.at[half, 0], yr.at[half, 1], zr.at[half, 0], zr.at[half, 1])[i]
+        remote(dst, dst, ss.at[half, i], rs.at[half, i], on_line(1)).wait_recv()
+
+    edge = top | bottom
+    side = jnp.where(top, half_way, -half_way)
+    to_relay = on_line(side)
+    telling = [
+        remote(pk.at[pl.ds(0, 5)], mk.at[pl.ds(3, 5)], ss.at[4, 0], rs.at[4, 0], to_relay),
+        remote(pk.at[pl.ds(5, 5)], mk.at[pl.ds(8, 5)], ss.at[4, 1], rs.at[4, 1], to_relay),
+        remote(u.at[0, jnp.where(top, 1, 0)], mu, ss.at[4, 2], rs.at[4, 2],
+               at(side, jnp.where(top, 0, low_n - 1))),
+        remote(pk.at[pl.ds(10, 1)], mk.at[pl.ds(13, 1)], ss.at[4, 3], rs.at[4, 3], to_relay),
+    ]
+    first = at(side, jnp.where(top, 0, low_n - 1))
+    second = at(side, jnp.where(top, 1, low_n - 2))
+    slot_first, slot_second = jnp.where(top, 0, 1), jnp.where(top, 2, 3)
+
+    def pass_layer(k, frm, count, to, sem, dev):
+        return remote(mk.at[pl.ds(frm, count)], e.at[pl.ds(to, count)], ss.at[5, k], rs.at[2, sem], dev)
+
+    passing = [
+        pass_layer(0, 16, 1, jnp.where(top, 3, 6), slot_first, first),
+        pass_layer(1, 16, 1, jnp.where(top, 1, 8), slot_second, second),
+        pass_layer(2, 13, 1, jnp.where(top, 2, 7), slot_first, first),
+        pass_layer(3, 13, 1, jnp.where(top, 0, 9), slot_second, second),
+        pass_layer(4, 14, 2, jnp.where(top, 0, 8), slot_second, first),
+    ]
 
     zero = jnp.zeros((8, 128), F32)
     loads[0].wait()
     loads[1].wait()
     hold(0, disp)
+    loads[3].wait()
+    loads[4].wait()
+    for c in range(3):
+        pk[c] = jnp.where(top, u[0, 0, c], u[0, 1, c])
+    pk[3] = jnp.where(top, emax[1], emax[0])
+    pk[4] = jnp.where(top, reg[1], reg[0]).astype(F32)
     pl.semaphore_wait(barrier, len(greet))
     faces = [send_faces(0)]
+
+    @pl.when(edge)
+    def _():
+        telling[2].start()
+        telling[0].start()
+
 
     steps = []
     reach = 1
@@ -203,12 +242,13 @@
             pl.semaphore_wait(dbl.at[s], 2)
 
     dbl_signal(0)
-    for c in loads[2:10]:
+    loads[2].wait()
+    for c in loads[5:10]:
         c.wait()
     hold(1, dold)
+    faces.append(send_faces(1))
     dbl_wait(0)
     dbl_signal(1)
-    pass_on(0)
 
     def pick(table, where_is):
         out = table[REGIONS - 1]
@@ -221,50 +261,108 @@
     ratio_c = [pick([ratio[k] for k in range(REGIONS)], is_region[l]) for l in range(2)]
     scale_c = [pick([scale[k] for k in range(REGIONS)], is_region[l]) for l in range(2)]
 
-    def strains(half):
+    def flats(half):
         from_lo = zr[half, 0] * zlo_on
         from_hi = zr[half, 1] * zhi_on
         out = []
         for l in range(2):
-            grad = [[None] * 3 for _ in range(3)]
+            grad_y, grad_z = [], []
             for c in range(3):
                 j = l * 3 + c
                 val = u[half, l, c]
-                prev_x = xr[half, 0, c] if l == 0 else u[half, 0, c]
-                next_x = xr[half, 1, c] if l == 1 else u[half, 1, c]
                 below = jnp.broadcast_to(yr[half, 0, j] * ylo_on, (8, 128))
                 above = jnp.broadcast_to(yr[half, 1, j] * yhi_on, (8, 128))
                 prev_y = pltpu.roll(jnp.where(row == 7, below, val), 1, 0)
                 next_y = pltpu.roll(jnp.where(row == 0, above, val), 7, 0)
                 prev_z = jnp.where(lane == 0, pltpu.roll(from_lo, (128 - j) % 128, 1), pltpu.roll(val, 1, 1))
                 next_z = jnp.where(lane == 127, pltpu.roll(from_hi, 127 - j, 1), pltpu.roll(val, 127, 1))
-                grad[0][c] = 0.5 * (next_x - prev_x)
-                grad[1][c] = 0.5 * (next_y - prev_y)
-                grad[2][c] = 0.5 * (next_z - prev_z)
-            out.append(deviator(grad))
+                grad_y.append(0.5 * (next_y - prev_y))
+                grad_z.append(0.5 * (next_z - prev_z))
+            out.append(flat_parts(grad_y, grad_z))
         return out
 
-    wait_faces(0)
+    def strains(half, flat):
+        out = []
+        for l in range(2):
+            grad_x = []
+            for c in range(3):
+                prev_x = xr[half, 0, c] if l == 0 else u[half, 0, c]
+                next_x = xr[half, 1, c] if l == 1 else u[half, 1, c]
+                grad_x.append(0.5 * (next_x - prev_x))
+            out.append(deviator(grad_x, flat[l]))
+        return out
+
+    def drive_of(d, g, r, m, most):
+        energy = g * (
+            d[0] * d[0] + d[1] * d[1] + d[2] * d[2] + 2.0 * (d[3] * d[3] + d[4] * d[4] + d[5] * d[5]))
+        peak = jnp.maximum(most, energy)
+        soft = 1.0 - lax.erf((peak - energy) / m) / r
+        return peak, soft, soft * energy
+
+    for i in range(2, 6):
+        wait_face(0, i)
+    flat_new = flats(0)
+    for i in range(5):
+        pk[5 + i] = jnp.where(top, flat_new[1][i], flat_new[0][i])
+
+    @pl.when(edge)
+    def _():
+        telling[1].start()
+
+    @pl.when(jnp.logical_not(bottom))
+    def _():
+        wait_face(0, 0)
+
+    @pl.when(jnp.logical_not(top))
+    def _():
+        wait_face(0, 1)
+
+    @pl.when(edge)
+    def _():
+        near = [xr[0, jnp.where(top, 0, 1), c] for c in range(3)]
+        grad_x = [0.5 * (jnp.where(top, u[0, 1, c], near[c]) - jnp.where(top, near[c], u[0, 0, c]))
+                  for c in range(3)]
+        flat = [jnp.where(top, flat_new[0][i], flat_new[1][i]) for i in range(5)]
+        both = [jnp.where(top, a, b) for a, b in (
+            (shear_c[0], shear_c[1]), (ratio_c[0], ratio_c[1]), (scale_c[0], scale_c[1]), (emax[0], emax[1]))]
+        pk[10] = drive_of(deviator(grad_x, flat), *both)[2]
+        telling[3].start()
+
+    dbl_wait(1)
+    dbl_signal(2)
+    pass_on(0)
+
+    @pl.when(edge)
+    def _():
+        for c in telling[:3]:
+            c.wait_recv()
+        grad_x = [0.5 * (jnp.where(top, mu[c], mk[3 + c]) - jnp.where(top, mk[3 + c], mu[c])) for c in range(3)]
+        theirs = [mk[7] == float(k) for k in range(REGIONS)]
+        both = [pick([t[k] for k in range(REGIONS)], theirs) for t in (shear, ratio, scale)]
+        mk[16] = drive_of(deviator(grad_x, [mk[8 + i] for i in range(5)]), *both, mk[6])[2]
+        passing[0].start()
+        passing[1].start()
+        telling[3].wait_recv()
+        passing[2].start()
+        passing[3].start()
+        remote(mk.at[pl.ds(14, 2)], mk.at[pl.ds(14, 2)], ss.at[4, 4], rs.at[4, 4], to_relay).wait_recv()
+        passing[4].start()
+
+    pass_on(1)
+
+    @pl.when(bottom)
+    def _():
+        wait_face(0, 0)
 
     @pl.when(top)
     def _():
-        signal(xok, on_x(-1))
-
-    @pl.when(bottom)
-    def _():
-        signal(xok, on_x(1))
-
-    dev_new = strains(0)
+        wait_face(0, 1)
+
+    dev_new = strains(0, flat_new)
     softening = []
     for l in range(2):
-        d = dev_new[l]
-        energy = shear_c[l] * (
-            d[0] * d[0] + d[1] * d[1] + d[2] * d[2] + 2.0 * (d[3] * d[3] + d[4] * d[4] + d[5] * d[5]))
-        peak = jnp.maximum(emax[l], energy)
-        soft = 1.0 - lax.erf((peak - energy) / scale_c[l]) / ratio_c[l]
-        enext[l] = peak
+        enext[l], soft, e[4 + l] = drive_of(dev_new[l], shear_c[l], ratio_c[l], scale_c[l], emax[l])
         softening.append(soft)
-        e[4 + l] = soft * energy
 
     own = e.at[pl.ds(4, 2)]
     wide = [
@@ -273,22 +371,15 @@
         remote(own, e.at[pl.ds(0, 2)], ss.at[2, 2], rs.at[2, 2], on_x(2)),
         remote(own, e.at[pl.ds(8, 2)], ss.at[2, 3], rs.at[2, 3], on_x(-2)),
     ]
-    for c in wide[:2]:
-        c.start()
-
-    @pl.when((low == low_n - 2) | (low == 1))
-    def _():
-        pl.semaphore_wait(xok, 1)
-
-    for c in wide[2:]:
-        c.start()
-    faces.append(send_faces(1))
-    dbl_wait(1)
-    dbl_signal(2)
-    pass_on(1)
+    under, above_ = low == low_n - 2, low == 1
+    spread = list(zip((jnp.logical_not(top), jnp.logical_not(bottom), low < low_n - 2, low > 1), wide))
+    spread.append((under | above_, remote(
+        own, mk.at[pl.ds(14, 2)], ss.at[4, 4], rs.at[4, 4],
+        at(jnp.where(under, half_way, -half_way), jnp.where(under, low_n - 1, 0)))))
+    for cond, c in reversed(spread):
+        pl.when(cond)(c.start)
     dbl_wait(2)
     dbl_signal(3)
-
 
     row_mask = jnp.where(row < 4, yhi_on, ylo_on)
     lane_mask = jnp.where(lane < 4, zhi_on, jnp.where(lane >= 124, zlo_on, 0.0))
@@ -394,9 +485,10 @@
     for d in order:
         c = remote(ts.at[0], tr.at[d - 1], ls_sem, lr_sem, on_line(d))
         c.start()
-    wait_faces(1)
+    for i in range(6):
+        wait_face(1, i)
     loads[10].wait()
-    dev_old = strains(1)
+    dev_old = strains(1, flats(1))
     jump = [[2.0 * shear_c[l] * (dev_new[l][a] - dev_old[l][a]) for a in range(6)] for l in range(2)]
     total = [[None] * 6 for _ in range(2)]
     for k in range(TERMS):
@@ -426,14 +518,19 @@
         acc = acc + tr[d]
     sums_out[...] = acc
 
-    for group in (faces[0], faces[1], wide, edges):
+    for group in (faces[0], faces[1], edges):
         for c in group:
             c.wait_send()
 
-    @pl.when(top | bottom)
+    for cond, c in spread:
+        pl.when(cond)(c.wait_send)
+
+    @pl.when(edge)
     def _():
         relay(0).wait_send()
         relay(1).wait_send()
+        for c in telling + passing:
+            c.wait_send()
 
     every.wait_send()
     along.wait_send()
@@ -495,8 +592,9 @@
                 vm((2, 8, 128), F32), vm((6, 8, 128), F32),
                 vm((1, 1, 128), F32), vm((plane_n - 1, 1, 128), F32),
                 vm((1, 1, 128), F32), vm((line_n - 1, 1, 128), F32),
-                dma((11,)), dma((4, 8)), dma((4, 8)), dma, dma, dma, dma,
-                pltpu.SemaphoreType.REGULAR((4,)), pltpu.SemaphoreType.REGULAR,
+                vm((11, 8, 128), F32), vm((17, 8, 128), F32), vm((3, 8, 128), F32),
+                dma((11,)), dma((6, 8)), dma((6, 8)), dma, dma, dma, dma,
+                pltpu.SemaphoreType.REGULAR((4,)),
             ],
             compiler_params=pltpu.CompilerParams(
                 collective_id=0, has_side_effects=True, vmem_limit_bytes=16 << 20),

time: 65.1 us -> 61.9 us (0.951)
  Pallas kernels: 64.2 us -> 61.1 us
    pallas_call x1, Pallas kernels: 63.4 us -> 60.3 us  [on_device(): pl.pallas_call(functools.partial(kernel, (nx, ny, nz, zhi)), out_shape=(s...]
where the time goes in v3:
time: 61.9 us; the launch traced here: 61.7 us
  Pallas kernels  61.1 us (99%)
  between operations  0.64 us (1%)
    pallas_call x1, Pallas kernels, on_device(): pl.pallas_call(functools.partial(kernel, (nx, ny, nz, zhi)), out_shape=(s...  60.3 us

profile of v3, /device:TPU:1, one launch (start us, length us, event | category | flops | bytes accessed | tf_op | source)
XLA Modules:
  0.0 61.7 jit_solution(15309498435216890187)
XLA Ops:
  0.6 60.3 %shard_map.146 = (f32[6,2,8,128]{3,2,1,0:T(8,128)S(1)}, f32[6,6,2,8,128]{4,3,2,1,0:T(8,128)S(1)}, f32[2,8,128]{2,1,0:T(8,128)S(1)}, f32[10,8,128]{2,1,0:T(8,128)S(1)}, f32[1,128]{1,0:T(1,128)S(1)}) custom-call(f32[3,2,8,128]{3,2,1,0:T(8,128)} %refs_0_.1, f32[3,2,8,128]{3,2,1,0:T(8,128)} %refs_1_.1, f32[6,6,2,8,128]{4,3,2,1,0:T(8,128)} %refs_2_.1, ...), custom_call_target="tpu_custom_call" | custom-call | tf_op jit(solution)/shard_map/pallas_call | solution.py:577
  60.9 0.8 %shard_map.147 = (f32[6,2,8,128]{3,2,1,0:T(8,128)}, f32[6,6,2,8,128]{4,3,2,1,0:T(8,128)}, f32[2,8,128]{2,1,0:T(8,128)}, f32[2,8,128]{2,1,0:T(8,128)}, f32[2,8,128]{2,1,0:T(8,128)}) custom-call(f32[6,2,8,128]{3,2,1,0:T(8,128)S(1)} %get-tuple-element.10.stress, f32[6,6,2,8,128]{4,3,2,1,0:T(8,128)S(1)} %get-tuple-element.11.vnext, ...), custom_call_target="tpu_custom_call" | custom-call | tf_op jit(solution)/shard_map/pallas_call | solution.py:602

commit v4 on v3

--- a/solution.py
+++ b/solution.py
@@ -80,25 +80,29 @@
      pk, mk, mu, ld_sem, ss, rs, ps_sem, pr_sem, ls_sem, lr_sem, dbl) = refs
 
     ix, iy, iz = lax.axis_index("gx"), lax.axis_index("gy"), lax.axis_index("gz")
-    low, hi = ix % low_n, ix // low_n
+    low, hi = lax.rem(ix, low_n), lax.div(ix, low_n)
     spot = hi * nz + iz
     place = low * ny + iy
     top = low == low_n - 1
     bottom = low == 0
 
+    def wrap(q, n):
+        return jnp.where(q >= n, q - n, q)
+
     def on_x(d):
-        return {"gx": (ix + d + nx) % nx, "gy": iy, "gz": iz}
+        return {"gx": wrap(ix + d % nx, nx), "gy": iy, "gz": iz}
 
     def at(d, low_to, dy=0):
-        q = (spot + d + line_n) % line_n
-        return {"gx": (q // nz) * low_n + low_to, "gy": (iy + dy + ny) % ny, "gz": q % nz}
+        q = wrap(spot + (d % line_n if isinstance(d, int) else d), line_n)
+        y_to = wrap(iy + dy % ny, ny) if dy else iy
+        return {"gx": lax.div(q, nz) * low_n + low_to, "gy": y_to, "gz": lax.rem(q, nz)}
 
     def on_line(d, dy=0):
         return at(d, low, dy)
 
     def on_plane(d):
-        q = (place + d) % plane_n
-        return {"gx": hi * low_n + q // ny, "gy": q % ny, "gz": iz}
+        q = wrap(place + d, plane_n)
+        return {"gx": hi * low_n + lax.div(q, ny), "gy": lax.rem(q, ny), "gz": iz}
 
     def either(cond, one, other):
         return {k: jnp.where(cond, one[k], other[k]) for k in one}
@@ -111,20 +115,20 @@
             src_ref=src, dst_ref=dst, send_sem=ssem, recv_sem=rsem,
             device_id=dev, device_id_type=pl.DeviceIdType.MESH)
 
-    loads = [pltpu.make_async_copy(a, b, ld_sem.at[i]) for i, (a, b) in enumerate(
-        ((dir_h, dirm), (disp_h, disp), (dold_h, dold), (reg_h, reg), (emax_h, emax),
-         (shear_h, shear), (ratio_h, ratio), (scale_h, scale), (moduli_h, moduli), (times_h, times),
-         (visc_h, visc)))]
+    loads = [pltpu.make_async_copy(a, b, ld_sem.at[i]) for i, a, b in (
+        (0, dir_h, dirm), (1, disp_h, disp), (4, dold_h, dold), (2, reg_h, reg), (3, emax_h, emax),
+        (0, shear_h, shear), (1, ratio_h, ratio), (2, scale_h, scale), (3, moduli_h, moduli), (5, times_h, times),
+        (4, visc_h, visc))]
     for c in loads[:2]:
         c.start()
 
     barrier = pltpu.get_barrier_semaphore()
-    greet = [at(s, (low + r + low_n) % low_n) for r in (0, 1, -1, 2, -2) for s in (half_way, -half_way)]
+    greet = [at(s, wrap(low + r % low_n, low_n)) for r in (0, 1, -1, 2, -2) for s in (half_way, -half_way)]
     greet += [on_plane(d) for d in range(1, plane_n)]
     greet += [on_line(1), on_line(-1)]
     for dev in greet:
         signal(barrier, dev)
-    for c in loads[2:]:
+    for c in loads[2:5]:
         c.start()
 
     row = lax.broadcasted_iota(jnp.int32, (8, 128), 0)
@@ -151,14 +155,14 @@
 
     def send_faces(half):
         out = [
-            remote(u.at[half, 1], xr.at[half, jnp.where(top, 2, 0)], ss.at[half, 0],
-                   rs.at[half, jnp.where(top, 6, 0)], either(top, on_line(half_way), on_x(1))),
-            remote(u.at[half, 0], xr.at[half, jnp.where(bottom, 2, 1)], ss.at[half, 1],
-                   rs.at[half, jnp.where(bottom, 6, 1)], either(bottom, on_line(-half_way), on_x(-1))),
-            remote(ys.at[half, 0], yr.at[half, 0], ss.at[half, 2], rs.at[half, 2], on_line(0, 1)),
-            remote(ys.at[half, 1], yr.at[half, 1], ss.at[half, 3], rs.at[half, 3], on_line(0, -1)),
-            remote(zs.at[half, 0], zr.at[half, 0], ss.at[half, 4], rs.at[half, 4], on_line(1)),
-            remote(zs.at[half, 1], zr.at[half, 1], ss.at[half, 5], rs.at[half, 5], on_line(-1)),
+            remote(u.at[half, 1], xr.at[half, jnp.where(top, 2, 0)], ss.at[0],
+                   rs.at[7 * half + jnp.where(top, 6, 0)], either(top, on_line(half_way), on_x(1))),
+            remote(u.at[half, 0], xr.at[half, jnp.where(bottom, 2, 1)], ss.at[1],
+                   rs.at[7 * half + jnp.where(bottom, 6, 1)], either(bottom, on_line(-half_way), on_x(-1))),
+            remote(ys.at[half, 0], yr.at[half, 0], ss.at[2], rs.at[7 * half + 2], on_line(0, 1)),
+            remote(ys.at[half, 1], yr.at[half, 1], ss.at[3], rs.at[7 * half + 3], on_line(0, -1)),
+            remote(zs.at[half, 0], zr.at[half, 0], ss.at[4], rs.at[7 * half + 4], on_line(1)),
+            remote(zs.at[half, 1], zr.at[half, 1], ss.at[5], rs.at[7 * half + 5], on_line(-1)),
         ]
         for c in out:
             c.start()
@@ -166,35 +170,35 @@
 
     def relay(half):
         side = jnp.where(top, 0, 1)
-        return remote(xr.at[half, 2], xr.at[half, side], ss.at[half, 6], rs.at[half, side],
+        return remote(xr.at[half, 2], xr.at[half, side], ss.at[6], rs.at[7 * half + side],
                       either(top, at(half_way, 0), at(-half_way, low_n - 1)))
 
     def pass_on(half):
         @pl.when(top | bottom)
         def _():
-            remote(xr.at[half, 2], xr.at[half, 2], ss.at[half, 6], rs.at[half, 6], on_line(1)).wait_recv()
+            remote(xr.at[half, 2], xr.at[half, 2], ss.at[6], rs.at[7 * half + 6], on_line(1)).wait_recv()
             relay(half).start()
 
     def wait_face(half, i):
         dst = (xr.at[half, 0], xr.at[half, 1], yr.at[half, 0], yr.at[half, 1], zr.at[half, 0], zr.at[half, 1])[i]
-        remote(dst, dst, ss.at[half, i], rs.at[half, i], on_line(1)).wait_recv()
+        remote(dst, dst, ss.at[i], rs.at[7 * half + i], on_line(1)).wait_recv()
 
     edge = top | bottom
-    side = jnp.where(top, half_way, -half_way)
+    side = jnp.where(top, half_way, line_n - half_way)
     to_relay = on_line(side)
     telling = [
-        remote(pk.at[pl.ds(0, 5)], mk.at[pl.ds(3, 5)], ss.at[4, 0], rs.at[4, 0], to_relay),
-        remote(pk.at[pl.ds(5, 5)], mk.at[pl.ds(8, 5)], ss.at[4, 1], rs.at[4, 1], to_relay),
-        remote(u.at[0, jnp.where(top, 1, 0)], mu, ss.at[4, 2], rs.at[4, 2],
+        remote(pk.at[pl.ds(0, 5)], mk.at[pl.ds(3, 5)], ss.at[11 + 0], rs.at[26 + 0], to_relay),
+        remote(pk.at[pl.ds(5, 5)], mk.at[pl.ds(8, 5)], ss.at[11 + 1], rs.at[26 + 1], to_relay),
+        remote(u.at[0, jnp.where(top, 1, 0)], mu, ss.at[11 + 2], rs.at[26 + 2],
                at(side, jnp.where(top, 0, low_n - 1))),
-        remote(pk.at[pl.ds(10, 1)], mk.at[pl.ds(13, 1)], ss.at[4, 3], rs.at[4, 3], to_relay),
+        remote(pk.at[pl.ds(10, 1)], mk.at[pl.ds(13, 1)], ss.at[11 + 3], rs.at[26 + 3], to_relay),
     ]
     first = at(side, jnp.where(top, 0, low_n - 1))
     second = at(side, jnp.where(top, 1, low_n - 2))
     slot_first, slot_second = jnp.where(top, 0, 1), jnp.where(top, 2, 3)
 
     def pass_layer(k, frm, count, to, sem, dev):
-        return remote(mk.at[pl.ds(frm, count)], e.at[pl.ds(to, count)], ss.at[5, k], rs.at[2, sem], dev)
+        return remote(mk.at[pl.ds(frm, count)], e.at[pl.ds(to, count)], ss.at[16 + k], rs.at[14 + sem], dev)
 
     passing = [
         pass_layer(0, 16, 1, jnp.where(top, 3, 6), slot_first, first),
@@ -222,6 +226,8 @@
         telling[2].start()
         telling[0].start()
 
+    for c in loads[5:10]:
+        c.start()
 
     steps = []
     reach = 1
@@ -243,10 +249,10 @@
 
     dbl_signal(0)
     loads[2].wait()
+    hold(1, dold)
+    loads[10].start()
     for c in loads[5:10]:
         c.wait()
-    hold(1, dold)
-    faces.append(send_faces(1))
     dbl_wait(0)
     dbl_signal(1)
 
@@ -345,10 +351,8 @@
         telling[3].wait_recv()
         passing[2].start()
         passing[3].start()
-        remote(mk.at[pl.ds(14, 2)], mk.at[pl.ds(14, 2)], ss.at[4, 4], rs.at[4, 4], to_relay).wait_recv()
+        remote(mk.at[pl.ds(14, 2)], mk.at[pl.ds(14, 2)], ss.at[11 + 4], rs.at[26 + 4], to_relay).wait_recv()
         passing[4].start()
-
-    pass_on(1)
 
     @pl.when(bottom)
     def _():
@@ -366,18 +370,21 @@
 
     own = e.at[pl.ds(4, 2)]
     wide = [
-        remote(own, e.at[pl.ds(2, 2)], ss.at[2, 0], rs.at[2, 0], on_x(1)),
-        remote(own, e.at[pl.ds(6, 2)], ss.at[2, 1], rs.at[2, 1], on_x(-1)),
-        remote(own, e.at[pl.ds(0, 2)], ss.at[2, 2], rs.at[2, 2], on_x(2)),
-        remote(own, e.at[pl.ds(8, 2)], ss.at[2, 3], rs.at[2, 3], on_x(-2)),
+        remote(own, e.at[pl.ds(2, 2)], ss.at[7 + 0], rs.at[14 + 0], on_x(1)),
+        remote(own, e.at[pl.ds(6, 2)], ss.at[7 + 1], rs.at[14 + 1], on_x(-1)),
+        remote(own, e.at[pl.ds(0, 2)], ss.at[7 + 2], rs.at[14 + 2], on_x(2)),
+        remote(own, e.at[pl.ds(8, 2)], ss.at[7 + 3], rs.at[14 + 3], on_x(-2)),
     ]
     under, above_ = low == low_n - 2, low == 1
     spread = list(zip((jnp.logical_not(top), jnp.logical_not(bottom), low < low_n - 2, low > 1), wide))
     spread.append((under | above_, remote(
-        own, mk.at[pl.ds(14, 2)], ss.at[4, 4], rs.at[4, 4],
-        at(jnp.where(under, half_way, -half_way), jnp.where(under, low_n - 1, 0)))))
+        own, mk.at[pl.ds(14, 2)], ss.at[11 + 4], rs.at[26 + 4],
+        at(jnp.where(under, half_way, line_n - half_way), jnp.where(under, low_n - 1, 0)))))
     for cond, c in reversed(spread):
         pl.when(cond)(c.start)
+    for c in faces[0]:
+        c.wait_send()
+    faces.append(send_faces(1))
     dbl_wait(2)
     dbl_signal(3)
 
@@ -401,15 +408,21 @@
     ezs[0] = to_hi
     ezs[1] = to_lo
     edges = [
-        remote(ezs.at[0], ezr.at[2], ss.at[3, 0], rs.at[3, 0], on_line(1, 1)),
-        remote(ezs.at[0], ezr.at[3], ss.at[3, 1], rs.at[3, 1], on_line(1, -1)),
-        remote(ezs.at[1], ezr.at[4], ss.at[3, 2], rs.at[3, 2], on_line(-1, 1)),
-        remote(ezs.at[1], ezr.at[5], ss.at[3, 3], rs.at[3, 3], on_line(-1, -1)),
-        remote(ezs.at[0], ezr.at[0], ss.at[3, 4], rs.at[3, 4], on_line(1)),
-        remote(ezs.at[1], ezr.at[1], ss.at[3, 5], rs.at[3, 5], on_line(-1)),
-        remote(eys.at[0], eyr.at[0], ss.at[3, 6], rs.at[3, 6], on_line(0, 1)),
-        remote(eys.at[1], eyr.at[1], ss.at[3, 7], rs.at[3, 7], on_line(0, -1)),
+        remote(ezs.at[0], ezr.at[2], ss.at[11 + 0], rs.at[18 + 0], on_line(1, 1)),
+        remote(ezs.at[0], ezr.at[3], ss.at[11 + 1], rs.at[18 + 1], on_line(1, -1)),
+        remote(ezs.at[1], ezr.at[4], ss.at[11 + 2], rs.at[18 + 2], on_line(-1, 1)),
+        remote(ezs.at[1], ezr.at[5], ss.at[11 + 3], rs.at[18 + 3], on_line(-1, -1)),
+        remote(ezs.at[0], ezr.at[0], ss.at[11 + 4], rs.at[18 + 4], on_line(1)),
+        remote(ezs.at[1], ezr.at[1], ss.at[11 + 5], rs.at[18 + 5], on_line(-1)),
+        remote(eys.at[0], eyr.at[0], ss.at[11 + 6], rs.at[18 + 6], on_line(0, 1)),
+        remote(eys.at[1], eyr.at[1], ss.at[11 + 7], rs.at[18 + 7], on_line(0, -1)),
     ]
+    @pl.when(edge)
+    def _():
+        for c in telling + passing:
+            c.wait_send()
+
+    pl.when(under | above_)(spread[4][1].wait_send)
     for c in edges:
         c.start()
     for c in edges[6:]:
@@ -475,6 +488,8 @@
         c = remote(gs.at[0], gp.at[d - 1], ps_sem, pr_sem, on_plane(d))
         c.start()
     every = remote(gp, gp, ps_sem, pr_sem, on_plane(1))
+    pl.when(edge)(relay(0).wait_send)
+    pass_on(1)
     every.wait_recv()
     acc = mine
     for d in range(plane_n - 1):
@@ -512,27 +527,18 @@
         for a in range(6):
             stress[a, l] = softening[l] * (factor * dev_new[l][a] + total[l][a])
 
+    for group in (faces[1], edges):
+        for c in group:
+            c.wait_send()
+    for cond, c in spread[:4]:
+        pl.when(cond)(c.wait_send)
+    pl.when(edge)(relay(1).wait_send)
+    every.wait_send()
     along = remote(tr, tr, ls_sem, lr_sem, on_line(1))
     along.wait_recv()
     for d in range(line_n - 1):
         acc = acc + tr[d]
     sums_out[...] = acc
-
-    for group in (faces[0], faces[1], edges):
-        for c in group:
-            c.wait_send()
-
-    for cond, c in spread:
-        pl.when(cond)(c.wait_send)
-
-    @pl.when(edge)
-    def _():
-        relay(0).wait_send()
-        relay(1).wait_send()
-        for c in telling + passing:
-            c.wait_send()
-
-    every.wait_send()
     along.wait_send()
 
 
@@ -593,7 +599,7 @@
                 vm((1, 1, 128), F32), vm((plane_n - 1, 1, 128), F32),
                 vm((1, 1, 128), F32), vm((line_n - 1, 1, 128), F32),
                 vm((11, 8, 128), F32), vm((17, 8, 128), F32), vm((3, 8, 128), F32),
-                dma((11,)), dma((6, 8)), dma((6, 8)), dma, dma, dma, dma,
+                dma((6,)), dma((21,)), dma((31,)), dma, dma, dma, dma,
                 pltpu.SemaphoreType.REGULAR((4,)),
             ],
             compiler_params=pltpu.CompilerParams(

time: 61.9 us -> 61.7 us (level)
  no operation moved by 1% of the time
where the time goes in v4:
time: 61.7 us; the launch traced here: 61.4 us
  Pallas kernels  60.7 us (98%)
  between operations  0.64 us (1%)
    pallas_call x1, Pallas kernels, on_device(): pl.pallas_call(functools.partial(kernel, (nx, ny, nz, zhi)), out_shape=(s...  59.9 us

profile of v4, /device:TPU:1, one launch (start us, length us, event | category | flops | bytes accessed | tf_op | source)
XLA Modules:
  0.0 61.4 jit_solution(6186628904312354638)
XLA Ops:
  0.6 59.9 %shard_map.146 = (f32[6,2,8,128]{3,2,1,0:T(8,128)S(1)}, f32[6,6,2,8,128]{4,3,2,1,0:T(8,128)S(1)}, f32[2,8,128]{2,1,0:T(8,128)S(1)}, f32[10,8,128]{2,1,0:T(8,128)S(1)}, f32[1,128]{1,0:T(1,128)S(1)}) custom-call(f32[3,2,8,128]{3,2,1,0:T(8,128)} %refs_0_.1, f32[3,2,8,128]{3,2,1,0:T(8,128)} %refs_1_.1, f32[6,6,2,8,128]{4,3,2,1,0:T(8,128)} %refs_2_.1, ...), custom_call_target="tpu_custom_call" | custom-call | tf_op jit(solution)/shard_map/pallas_call | solution.py:583
  60.6 0.8 %shard_map.147 = (f32[6,2,8,128]{3,2,1,0:T(8,128)}, f32[6,6,2,8,128]{4,3,2,1,0:T(8,128)}, f32[2,8,128]{2,1,0:T(8,128)}, f32[2,8,128]{2,1,0:T(8,128)}, f32[2,8,128]{2,1,0:T(8,128)}) custom-call(f32[6,2,8,128]{3,2,1,0:T(8,128)S(1)} %get-tuple-element.10.stress, f32[6,6,2,8,128]{4,3,2,1,0:T(8,128)S(1)} %get-tuple-element.11.vnext, ...), custom_call_target="tpu_custom_call" | custom-call | tf_op jit(solution)/shard_map/pallas_call | solution.py:608

commit v5 on v4

--- a/solution.py
+++ b/solution.py
@@ -119,7 +119,7 @@
         (0, dir_h, dirm), (1, disp_h, disp), (4, dold_h, dold), (2, reg_h, reg), (3, emax_h, emax),
         (0, shear_h, shear), (1, ratio_h, ratio), (2, scale_h, scale), (3, moduli_h, moduli), (5, times_h, times),
         (4, visc_h, visc))]
-    for c in loads[:2]:
+    for c in loads[:5]:
         c.start()
 
     barrier = pltpu.get_barrier_semaphore()
@@ -128,8 +128,6 @@
     greet += [on_line(1), on_line(-1)]
     for dev in greet:
         signal(barrier, dev)
-    for c in loads[2:5]:
-        c.start()
 
     row = lax.broadcasted_iota(jnp.int32, (8, 128), 0)
     lane = lax.broadcasted_iota(jnp.int32, (8, 128), 1)
@@ -484,7 +482,7 @@
 
     gs[0] = mine
     sends = []
-    for d in range(1, plane_n):
+    for d in sorted(range(1, plane_n), key=lambda d: -min(d, plane_n - d)):
         c = remote(gs.at[0], gp.at[d - 1], ps_sem, pr_sem, on_plane(d))
         c.start()
     every = remote(gp, gp, ps_sem, pr_sem, on_plane(1))

time: 61.7 us -> 61.6 us (level)
  no operation moved by 1% of the time
where the time goes in v5:
time: 61.6 us; the launch traced here: 61.4 us
  Pallas kernels  60.8 us (99%)
  between operations  0.64 us (1%)
    pallas_call x1, Pallas kernels, on_device(): pl.pallas_call(functools.partial(kernel, (nx, ny, nz, zhi)), out_shape=(s...  60 us

profile of v5, /device:TPU:1, one launch (start us, length us, event | category | flops | bytes accessed | tf_op | source)
XLA Modules:
  0.0 61.4 jit_solution(7728908724656814315)
XLA Ops:
  0.6 60.0 %shard_map.146 = (f32[6,2,8,128]{3,2,1,0:T(8,128)S(1)}, f32[6,6,2,8,128]{4,3,2,1,0:T(8,128)S(1)}, f32[2,8,128]{2,1,0:T(8,128)S(1)}, f32[10,8,128]{2,1,0:T(8,128)S(1)}, f32[1,128]{1,0:T(1,128)S(1)}) custom-call(f32[3,2,8,128]{3,2,1,0:T(8,128)} %refs_0_.1, f32[3,2,8,128]{3,2,1,0:T(8,128)} %refs_1_.1, f32[6,6,2,8,128]{4,3,2,1,0:T(8,128)} %refs_2_.1, ...), custom_call_target="tpu_custom_call" | custom-call | tf_op jit(solution)/shard_map/pallas_call | solution.py:581
  60.6 0.8 %shard_map.147 = (f32[6,2,8,128]{3,2,1,0:T(8,128)}, f32[6,6,2,8,128]{4,3,2,1,0:T(8,128)}, f32[2,8,128]{2,1,0:T(8,128)}, f32[2,8,128]{2,1,0:T(8,128)}, f32[2,8,128]{2,1,0:T(8,128)}) custom-call(f32[6,2,8,128]{3,2,1,0:T(8,128)S(1)} %get-tuple-element.10.stress, f32[6,6,2,8,128]{4,3,2,1,0:T(8,128)S(1)} %get-tuple-element.11.vnext, ...), custom_call_target="tpu_custom_call" | custom-call | tf_op jit(solution)/shard_map/pallas_call | solution.py:606
